TPU v7x, 32 devices: a whole 2x2x4 slice. The times are simulated.
32 devices in a mesh: along: 8 (over y, x, core), across: 4 (over z).
Axes of the slice: x: 2, y: 2, z: 4, core: 2. Of those that a mesh axis runs over, the one named last changes fastest.
Arguments:
- fields: float32 [40, 3, 32, 4096], P(None, None, 'across', 'along'), may hold values from -6 to 6
- first_feet: int32 [32, 4096], P('across', 'along'), may hold values from 0 to 131071, as said below
- first_fraction: float32 [40, 32, 4096], P(None, 'across', 'along'), may hold values from 0 to 1
- second_feet: int32 [32, 4096], P('across', 'along'), may hold values from 0 to 131071, as said below
- second_fraction: float32 [40, 32, 4096], P(None, 'across', 'along'), may hold values from 0 to 1
- lateral_mix: float32 [32, 4096], P('across', 'along'), may hold values from 0.02 to 0.2
- vertical_mix: float32 [2, 39, 32, 4096], P(None, None, 'across', 'along'), may hold values from 0.05 to 5
- bottom_drag: float32 [32, 4096], P('across', 'along'), may hold values from 0.05 to 2
- surface_stress: float32 [2, 32, 4096], P(None, 'across', 'along'), may hold values from -3 to 3
Outputs:
- advanced: float32 [40, 3, 32, 4096], P(None, None, 'across', 'along')
Inputs may be any that keep to these rules, and one draw needn't show every extreme that they name: `first_feet`: A cell in the block of 8 x 512 cells with along block index a has its foot point (row p // 4096, column p % 4096) in a block whose along index lies from w to w + 1 - 1, w = max(a - 1 + 1, 0), at any cross block index. At most 1152 cells of one block have foot points in one block, and some pair of blocks reaches 1152. `second_feet`: as for first_feet.
All inputs are finite; a program needn't handle non-finite values.
Results may differ from a plain program's by a relative error of at most 0.00002.
Values sent between devices are 32-bit elements; how exact they have to be, the bound alone decides.
A program may use at most 64 MiB of HBM per device.

v0:
```python
import jax
import jax.numpy as jnp
from jax import lax
from jax.sharding import PartitionSpec as P


def shifted(block, axis, distance):
    devices = range(lax.axis_size(axis))
    route = [(i - distance, i) for i in devices if i - distance in devices]
    return lax.ppermute(block, axis, route)


def padded_2(value, sides, width):
    for axis, dim in sides:
        count, length = (lax.axis_size(axis), value.shape[dim])
        up = [(i, (i + 1) % count) for i in range(count - 1)]
        down = [(j, i) for i, j in up]
        last = lax.slice_in_dim(value, length - width, length, axis=dim)
        first = lax.slice_in_dim(value, 0, width, axis=dim)
        before = lax.ppermute(last, axis, up)
        after = lax.ppermute(first, axis, down)
        value = jnp.concatenate([before, value, after], axis=dim)
    return value


def interpolate(columns, fraction):
    upper = jnp.concatenate([columns[1:], columns[-1:]], axis=0)
    weight = fraction[:, None]
    return (1.0 - weight) * columns + weight * upper


def neighbour_sum(padded):
    total = padded[:, :, :-2, 1:-1] + padded[:, :, 2:, 1:-1]
    return total + padded[:, :, 1:-1, :-2] + padded[:, :, 1:-1, 2:]


def solve_columns(forcing, vertical_mix, bottom_drag, surface_stress):
    layers = forcing.shape[0]
    coupling = jnp.stack([vertical_mix[0], vertical_mix[0], vertical_mix[1]], axis=1)
    nothing = jnp.zeros_like(coupling[:1])
    below = jnp.concatenate([nothing, coupling], axis=0)
    above = jnp.concatenate([coupling, nothing], axis=0)
    friction = jnp.stack([bottom_drag, bottom_drag, jnp.zeros_like(bottom_drag)], axis=0)
    diagonal = (1.0 + below + above).at[0].add(friction)
    source = forcing.at[layers - 1, 0:2].add(surface_stress)
    factor = above[0] / diagonal[0]
    partial_value = source[0] / diagonal[0]
    factors = [factor]
    partials = [partial_value]
    for level_index in range(1, layers):
        denominator = diagonal[level_index] - below[level_index] * factor
        factor = above[level_index] / denominator
        partial_value = (source[level_index] + below[level_index] * partial_value) / denominator
        factors.append(factor)
        partials.append(partial_value)
    solution = partials[layers - 1]
    results = [solution]
    for level_index in range(layers - 2, -1, -1):
        solution = partials[level_index] + factors[level_index] * solution
        results.append(solution)
    return jnp.stack(results[::-1], axis=0)


def owners(feet, cross_dev, along_dev, along_total):
    flat_feet = feet.reshape(-1)
    global_row = flat_feet // along_total
    global_column = flat_feet % along_total
    local_cell = global_row % cross_dev * along_dev + global_column % along_dev
    return (global_column // along_dev, global_row // cross_dev, local_cell)


def slot_position(partner):
    order = jnp.argsort(partner, stable=True)
    sorted_partner = partner[order]
    first = jnp.searchsorted(sorted_partner, sorted_partner, side="left")
    ranked = jnp.arange(partner.shape[0], dtype=jnp.int32) - first
    return jnp.zeros_like(partner).at[order].set(ranked)


def hop_groups(reach, power):
    upward = [offset + reach - 1 for offset in range(1 - reach, 0) if -offset >> power & 1]
    downward = [offset + reach - 1 for offset in range(1, reach) if offset >> power & 1]
    return (upward, downward)


def request_hop(message, steps):
    return shifted(message, "along", steps)


def column_hop(message, steps):
    return shifted(message, "along", steps)


def fetch(table, feet, cross_dev, along_dev):
    along_count = lax.axis_size("along")
    across_count = lax.axis_size("across")
    reach = along_count // 8
    capacity = 9 * cross_dev * along_dev // (8 * across_count * reach)
    width = table.shape[1]
    owner_along, owner_across, local_cell = owners(
        feet, cross_dev, along_dev, along_dev * along_count
    )
    partner = owner_along * across_count + owner_across
    position = slot_position(partner)
    span = 2 * reach - 1
    offset = owner_along - lax.axis_index("along")
    target = (owner_across * span + offset + reach - 1) * capacity + position
    requests = jnp.zeros((across_count * span * capacity,), jnp.int32).at[target].set(local_cell)
    requests = requests.reshape(across_count, span, capacity)
    moved = lax.all_to_all(requests, "across", split_axis=0, concat_axis=0, tiled=True)
    bit_count = (reach - 1).bit_length()
    for power in range(bit_count):
        upward, downward = hop_groups(reach, power)
        moved = moved.at[:, upward].set(request_hop(moved[:, upward], -(1 << power)))
        moved = moved.at[:, downward].set(request_hop(moved[:, downward], 1 << power))
    picked = jnp.take(table, moved.reshape(-1), axis=0).reshape(across_count, span, capacity, width)
    for power in range(bit_count):
        upward, downward = hop_groups(reach, power)
        picked = picked.at[:, upward].set(column_hop(picked[:, upward], 1 << power))
        picked = picked.at[:, downward].set(column_hop(picked[:, downward], -(1 << power)))
    returned = lax.all_to_all(picked, "across", split_axis=0, concat_axis=0, tiled=True)
    return jnp.take(returned.reshape(-1, width), target, axis=0)


def body(
    fields,
    first_feet,
    first_fraction,
    second_feet,
    second_fraction,
    lateral_mix,
    vertical_mix,
    bottom_drag,
    surface_stress,
):
    layers, components, cross_dev, along_dev = fields.shape
    row_count = layers * components
    width = (row_count + 127) // 128 * 128

    def advect(current, feet, fraction):
        table = current.reshape(row_count, cross_dev * along_dev).T
        table = jnp.pad(table, ((0, 0), (0, width - row_count)))
        gathered = fetch(table, feet, cross_dev, along_dev)[:, :row_count].T
        return interpolate(gathered.reshape(layers, components, cross_dev, along_dev), fraction)

    middle = advect(fields, first_feet, first_fraction)
    moved = advect(middle, second_feet, second_fraction)
    padded = padded_2(moved, (("across", 2), ("along", 3)), 1)
    beside_all = neighbour_sum(padded)
    row_total = cross_dev * lax.axis_size("across")
    column_total = along_dev * lax.axis_size("along")
    row_index = lax.axis_index("across") * cross_dev + jnp.arange(cross_dev, dtype=jnp.int32)
    column_index = lax.axis_index("along") * along_dev + jnp.arange(along_dev, dtype=jnp.int32)
    row_present = (row_index > 0).astype(jnp.float32) + (row_index < row_total - 1).astype(
        jnp.float32
    )
    column_present = (column_index > 0).astype(jnp.float32) + (
        column_index < column_total - 1
    ).astype(jnp.float32)
    present = row_present[:, None] + column_present[None, :]
    mixed = moved + lateral_mix * (beside_all - present * moved)
    return solve_columns(mixed, vertical_mix, bottom_drag, surface_stress)


def solution(mesh):
    in_specs = (
        P(None, None, "across", "along"),
        P("across", "along"),
        P(None, "across", "along"),
        P("across", "along"),
        P(None, "across", "along"),
        P("across", "along"),
        P(None, None, "across", "along"),
        P("across", "along"),
        P(None, "across", "along"),
    )
    out_specs = P(None, None, "across", "along")
    return jax.shard_map(body, mesh=mesh, in_specs=in_specs, out_specs=out_specs, check_vma=False)
```

profile of v0, /device:TPU:4, one launch (start us, length us, event | category | flops | bytes accessed | tf_op | source)
XLA Modules:
  0.0 987.6 jit_solution(13568579420459140786)
XLA Ops:
  0.8 5.8 sort.31
  6.6 23.0 %gather_fusion.2 = s32[4096]{0:T(1024)S(1)} fusion(s32[4096]{0:T(1024)S(1)} %get-tuple-element.337, s32[4096]{0:T(1024)S(1)} %get-tuple-element.338), kind=kCustom, calls=%fused_computation.6 | custom fusion | bytes 49152 | tf_op jit(solution)/shard_map/gather | solution.py:74
  29.6 300.6 %while.41 = (s32[]{:T(128)}, u32[4096]{0:T(1024)S(1)}, u32[4096]{0:T(1024)S(1)}, s32[4096]{0:T(1024)S(1)}, s32[]{:T(128)}, /*index=5*/s32[]{:T(128)}, s32[]{}) while((s32[]{:T(128)}, u32[4096]{0:T(1024)S(1)}, u32[4096]{0:T(1024)S(1)}, s32[4096]{0:T(1024)S(1)}, s32[]{:T(128)}, /*index=5*/s32[]{:T(128)}, s32[]{}) %tuple.182), condition=%wide.region_2.3_spmd.clone, body=%wide.region_1.2_spmd.clone.sunk | while | flops 77828 | bytes 270437 | solution.py:75
  29.6 23.0 %gather_fusion = s32[4096]{0:T(1024)S(1)} fusion(s32[4096]{0:T(1024)S(1)} %get-tuple-element.438, u32[4096]{0:T(1024)S(1)} %broadcast_clamp_fusion.8), kind=kCustom, calls=%fused_computation.clone.clone.1 | custom fusion | bytes 49152 | tf_op jit(solution)/shard_map/jit(searchsorted)/jit(_searchsorted_scan_impl)/vmap(jit(_searchsorted_scan_impl))/while/body/eval_jaxpr/gather | solution.py:75
  52.8 23.0 %gather_fusion = s32[4096]{0:T(1024)S(1)} fusion(s32[4096]{0:T(1024)S(1)} %get-tuple-element.438, u32[4096]{0:T(1024)S(1)} %broadcast_clamp_fusion.8), kind=kCustom, calls=%fused_computation.clone.clone.1 | custom fusion | bytes 49152 | tf_op jit(solution)/shard_map/jit(searchsorted)/jit(_searchsorted_scan_impl)/vmap(jit(_searchsorted_scan_impl))/while/body/eval_jaxpr/gather | solution.py:75
  75.9 23.0 %gather_fusion = s32[4096]{0:T(1024)S(1)} fusion(s32[4096]{0:T(1024)S(1)} %get-tuple-element.438, u32[4096]{0:T(1024)S(1)} %broadcast_clamp_fusion.8), kind=kCustom, calls=%fused_computation.clone.clone.1 | custom fusion | bytes 49152 | tf_op jit(solution)/shard_map/jit(searchsorted)/jit(_searchsorted_scan_impl)/vmap(jit(_searchsorted_scan_impl))/while/body/eval_jaxpr/gather | solution.py:75
  99.0 23.0 %gather_fusion = s32[4096]{0:T(1024)S(1)} fusion(s32[4096]{0:T(1024)S(1)} %get-tuple-element.438, u32[4096]{0:T(1024)S(1)} %broadcast_clamp_fusion.8), kind=kCustom, calls=%fused_computation.clone.clone.1 | custom fusion | bytes 49152 | tf_op jit(solution)/shard_map/jit(searchsorted)/jit(_searchsorted_scan_impl)/vmap(jit(_searchsorted_scan_impl))/while/body/eval_jaxpr/gather | solution.py:75
  122.2 23.0 %gather_fusion = s32[4096]{0:T(1024)S(1)} fusion(s32[4096]{0:T(1024)S(1)} %get-tuple-element.438, u32[4096]{0:T(1024)S(1)} %broadcast_clamp_fusion.8), kind=kCustom, calls=%fused_computation.clone.clone.1 | custom fusion | bytes 49152 | tf_op jit(solution)/shard_map/jit(searchsorted)/jit(_searchsorted_scan_impl)/vmap(jit(_searchsorted_scan_impl))/while/body/eval_jaxpr/gather | solution.py:75
  145.3 23.0 %gather_fusion = s32[4096]{0:T(1024)S(1)} fusion(s32[4096]{0:T(1024)S(1)} %get-tuple-element.438, u32[4096]{0:T(1024)S(1)} %broadcast_clamp_fusion.8), kind=kCustom, calls=%fused_computation.clone.clone.1 | custom fusion | bytes 49152 | tf_op jit(solution)/shard_map/jit(searchsorted)/jit(_searchsorted_scan_impl)/vmap(jit(_searchsorted_scan_impl))/while/body/eval_jaxpr/gather | solution.py:75
  168.4 23.0 %gather_fusion = s32[4096]{0:T(1024)S(1)} fusion(s32[4096]{0:T(1024)S(1)} %get-tuple-element.438, u32[4096]{0:T(1024)S(1)} %broadcast_clamp_fusion.8), kind=kCustom, calls=%fused_computation.clone.clone.1 | custom fusion | bytes 49152 | tf_op jit(solution)/shard_map/jit(searchsorted)/jit(_searchsorted_scan_impl)/vmap(jit(_searchsorted_scan_impl))/while/body/eval_jaxpr/gather | solution.py:75
  191.5 23.0 %gather_fusion = s32[4096]{0:T(1024)S(1)} fusion(s32[4096]{0:T(1024)S(1)} %get-tuple-element.438, u32[4096]{0:T(1024)S(1)} %broadcast_clamp_fusion.8), kind=kCustom, calls=%fused_computation.clone.clone.1 | custom fusion | bytes 49152 | tf_op jit(solution)/shard_map/jit(searchsorted)/jit(_searchsorted_scan_impl)/vmap(jit(_searchsorted_scan_impl))/while/body/eval_jaxpr/gather | solution.py:75
  214.7 23.0 %gather_fusion = s32[4096]{0:T(1024)S(1)} fusion(s32[4096]{0:T(1024)S(1)} %get-tuple-element.438, u32[4096]{0:T(1024)S(1)} %broadcast_clamp_fusion.8), kind=kCustom, calls=%fused_computation.clone.clone.1 | custom fusion | bytes 49152 | tf_op jit(solution)/shard_map/jit(searchsorted)/jit(_searchsorted_scan_impl)/vmap(jit(_searchsorted_scan_impl))/while/body/eval_jaxpr/gather | solution.py:75
  237.8 23.0 %gather_fusion = s32[4096]{0:T(1024)S(1)} fusion(s32[4096]{0:T(1024)S(1)} %get-tuple-element.438, u32[4096]{0:T(1024)S(1)} %broadcast_clamp_fusion.8), kind=kCustom, calls=%fused_computation.clone.clone.1 | custom fusion | bytes 49152 | tf_op jit(solution)/shard_map/jit(searchsorted)/jit(_searchsorted_scan_impl)/vmap(jit(_searchsorted_scan_impl))/while/body/eval_jaxpr/gather | solution.py:75
  260.9 23.0 %gather_fusion = s32[4096]{0:T(1024)S(1)} fusion(s32[4096]{0:T(1024)S(1)} %get-tuple-element.438, u32[4096]{0:T(1024)S(1)} %broadcast_clamp_fusion.8), kind=kCustom, calls=%fused_computation.clone.clone.1 | custom fusion | bytes 49152 | tf_op jit(solution)/shard_map/jit(searchsorted)/jit(_searchsorted_scan_impl)/vmap(jit(_searchsorted_scan_impl))/while/body/eval_jaxpr/gather | solution.py:75
  284.0 23.0 %gather_fusion = s32[4096]{0:T(1024)S(1)} fusion(s32[4096]{0:T(1024)S(1)} %get-tuple-element.438, u32[4096]{0:T(1024)S(1)} %broadcast_clamp_fusion.8), kind=kCustom, calls=%fused_computation.clone.clone.1 | custom fusion | bytes 49152 | tf_op jit(solution)/shard_map/jit(searchsorted)/jit(_searchsorted_scan_impl)/vmap(jit(_searchsorted_scan_impl))/while/body/eval_jaxpr/gather | solution.py:75
  307.2 23.0 %gather_fusion = s32[4096]{0:T(1024)S(1)} fusion(s32[4096]{0:T(1024)S(1)} %get-tuple-element.438, u32[4096]{0:T(1024)S(1)} %broadcast_clamp_fusion.8), kind=kCustom, calls=%fused_computation.clone.clone.1 | custom fusion | bytes 49152 | tf_op jit(solution)/shard_map/jit(searchsorted)/jit(_searchsorted_scan_impl)/vmap(jit(_searchsorted_scan_impl))/while/body/eval_jaxpr/gather | solution.py:75
  330.3 15.5 %scatter_custom_fusion = s32[4096]{0:T(1024)S(1)} fusion(s32[4096]{0:T(1024)S(1)} %get-tuple-element.339, s32[4096]{0:T(1024)S(1)} %convert_subtract_fusion.1, s32[]{:T(128)} %constant.249.clone.1), kind=kCustom, calls=%fused_computation.371 | custom fusion | bytes 16388 | tf_op jit(solution)/shard_map/scatter | solution.py:77
  345.9 15.5 %scatter_custom_fusion.1 = s32[4608]{0:T(1024)S(1)} fusion(s32[4096]{0:T(1024)S(1)} %get-tuple-element.325, s32[4096]{0:T(1024)S(1)} %get-tuple-element.336, s32[]{:T(128)} %constant.249.clone.1), kind=kCustom, calls=%fused_computation.362 | custom fusion | bytes 18436 | tf_op jit(solution)/shard_map/scatter | solution.py:108
  362.0 4.9 all-to-all-start
  367.0 5.8 sort.32
  372.8 23.0 %gather_fusion.3 = s32[4096]{0:T(1024)S(1)} fusion(s32[4096]{0:T(1024)S(1)} %get-tuple-element.333, s32[4096]{0:T(1024)S(1)} %get-tuple-element.334), kind=kCustom, calls=%fused_computation.7 | custom fusion | bytes 49152 | tf_op jit(solution)/shard_map/gather | solution.py:74
  395.8 300.6 %while.42 = (s32[]{:T(128)}, u32[4096]{0:T(1024)S(1)}, u32[4096]{0:T(1024)S(1)}, s32[4096]{0:T(1024)S(1)}, s32[]{:T(128)}, /*index=5*/s32[]{:T(128)}, s32[]{}) while((s32[]{:T(128)}, u32[4096]{0:T(1024)S(1)}, u32[4096]{0:T(1024)S(1)}, s32[4096]{0:T(1024)S(1)}, s32[]{:T(128)}, /*index=5*/s32[]{:T(128)}, s32[]{}) %tuple.179), condition=%wide.region_7.10_spmd.clone, body=%wide.region_6.9_spmd.clone.sunk | while | flops 77828 | bytes 270437 | solution.py:75
  395.8 23.0 %gather_fusion.1 = s32[4096]{0:T(1024)S(1)} fusion(s32[4096]{0:T(1024)S(1)} %get-tuple-element.417, u32[4096]{0:T(1024)S(1)} %broadcast_clamp_fusion.9), kind=kCustom, calls=%fused_computation.3.clone.clone.1 | custom fusion | bytes 49152 | tf_op jit(solution)/shard_map/jit(searchsorted)/jit(_searchsorted_scan_impl)/vmap(jit(_searchsorted_scan_impl))/while/body/eval_jaxpr/gather | solution.py:75
  419.0 23.0 %gather_fusion.1 = s32[4096]{0:T(1024)S(1)} fusion(s32[4096]{0:T(1024)S(1)} %get-tuple-element.417, u32[4096]{0:T(1024)S(1)} %broadcast_clamp_fusion.9), kind=kCustom, calls=%fused_computation.3.clone.clone.1 | custom fusion | bytes 49152 | tf_op jit(solution)/shard_map/jit(searchsorted)/jit(_searchsorted_scan_impl)/vmap(jit(_searchsorted_scan_impl))/while/body/eval_jaxpr/gather | solution.py:75
  442.1 23.0 %gather_fusion.1 = s32[4096]{0:T(1024)S(1)} fusion(s32[4096]{0:T(1024)S(1)} %get-tuple-element.417, u32[4096]{0:T(1024)S(1)} %broadcast_clamp_fusion.9), kind=kCustom, calls=%fused_computation.3.clone.clone.1 | custom fusion | bytes 49152 | tf_op jit(solution)/shard_map/jit(searchsorted)/jit(_searchsorted_scan_impl)/vmap(jit(_searchsorted_scan_impl))/while/body/eval_jaxpr/gather | solution.py:75
  465.2 23.0 %gather_fusion.1 = s32[4096]{0:T(1024)S(1)} fusion(s32[4096]{0:T(1024)S(1)} %get-tuple-element.417, u32[4096]{0:T(1024)S(1)} %broadcast_clamp_fusion.9), kind=kCustom, calls=%fused_computation.3.clone.clone.1 | custom fusion | bytes 49152 | tf_op jit(solution)/shard_map/jit(searchsorted)/jit(_searchsorted_scan_impl)/vmap(jit(_searchsorted_scan_impl))/while/body/eval_jaxpr/gather | solution.py:75
  488.3 23.0 %gather_fusion.1 = s32[4096]{0:T(1024)S(1)} fusion(s32[4096]{0:T(1024)S(1)} %get-tuple-element.417, u32[4096]{0:T(1024)S(1)} %broadcast_clamp_fusion.9), kind=kCustom, calls=%fused_computation.3.clone.clone.1 | custom fusion | bytes 49152 | tf_op jit(solution)/shard_map/jit(searchsorted)/jit(_searchsorted_scan_impl)/vmap(jit(_searchsorted_scan_impl))/while/body/eval_jaxpr/gather | solution.py:75
  511.5 23.0 %gather_fusion.1 = s32[4096]{0:T(1024)S(1)} fusion(s32[4096]{0:T(1024)S(1)} %get-tuple-element.417, u32[4096]{0:T(1024)S(1)} %broadcast_clamp_fusion.9), kind=kCustom, calls=%fused_computation.3.clone.clone.1 | custom fusion | bytes 49152 | tf_op jit(solution)/shard_map/jit(searchsorted)/jit(_searchsorted_scan_impl)/vmap(jit(_searchsorted_scan_impl))/while/body/eval_jaxpr/gather | solution.py:75
  534.6 23.0 %gather_fusion.1 = s32[4096]{0:T(1024)S(1)} fusion(s32[4096]{0:T(1024)S(1)} %get-tuple-element.417, u32[4096]{0:T(1024)S(1)} %broadcast_clamp_fusion.9), kind=kCustom, calls=%fused_computation.3.clone.clone.1 | custom fusion | bytes 49152 | tf_op jit(solution)/shard_map/jit(searchsorted)/jit(_searchsorted_scan_impl)/vmap(jit(_searchsorted_scan_impl))/while/body/eval_jaxpr/gather | solution.py:75
  557.7 23.0 %gather_fusion.1 = s32[4096]{0:T(1024)S(1)} fusion(s32[4096]{0:T(1024)S(1)} %get-tuple-element.417, u32[4096]{0:T(1024)S(1)} %broadcast_clamp_fusion.9), kind=kCustom, calls=%fused_computation.3.clone.clone.1 | custom fusion | bytes 49152 | tf_op jit(solution)/shard_map/jit(searchsorted)/jit(_searchsorted_scan_impl)/vmap(jit(_searchsorted_scan_impl))/while/body/eval_jaxpr/gather | solution.py:75
  580.9 23.0 %gather_fusion.1 = s32[4096]{0:T(1024)S(1)} fusion(s32[4096]{0:T(1024)S(1)} %get-tuple-element.417, u32[4096]{0:T(1024)S(1)} %broadcast_clamp_fusion.9), kind=kCustom, calls=%fused_computation.3.clone.clone.1 | custom fusion | bytes 49152 | tf_op jit(solution)/shard_map/jit(searchsorted)/jit(_searchsorted_scan_impl)/vmap(jit(_searchsorted_scan_impl))/while/body/eval_jaxpr/gather | solution.py:75
  604.0 23.0 %gather_fusion.1 = s32[4096]{0:T(1024)S(1)} fusion(s32[4096]{0:T(1024)S(1)} %get-tuple-element.417, u32[4096]{0:T(1024)S(1)} %broadcast_clamp_fusion.9), kind=kCustom, calls=%fused_computation.3.clone.clone.1 | custom fusion | bytes 49152 | tf_op jit(solution)/shard_map/jit(searchsorted)/jit(_searchsorted_scan_impl)/vmap(jit(_searchsorted_scan_impl))/while/body/eval_jaxpr/gather | solution.py:75
  627.1 23.0 %gather_fusion.1 = s32[4096]{0:T(1024)S(1)} fusion(s32[4096]{0:T(1024)S(1)} %get-tuple-element.417, u32[4096]{0:T(1024)S(1)} %broadcast_clamp_fusion.9), kind=kCustom, calls=%fused_computation.3.clone.clone.1 | custom fusion | bytes 49152 | tf_op jit(solution)/shard_map/jit(searchsorted)/jit(_searchsorted_scan_impl)/vmap(jit(_searchsorted_scan_impl))/while/body/eval_jaxpr/gather | solution.py:75
  650.2 23.0 %gather_fusion.1 = s32[4096]{0:T(1024)S(1)} fusion(s32[4096]{0:T(1024)S(1)} %get-tuple-element.417, u32[4096]{0:T(1024)S(1)} %broadcast_clamp_fusion.9), kind=kCustom, calls=%fused_computation.3.clone.clone.1 | custom fusion | bytes 49152 | tf_op jit(solution)/shard_map/jit(searchsorted)/jit(_searchsorted_scan_impl)/vmap(jit(_searchsorted_scan_impl))/while/body/eval_jaxpr/gather | solution.py:75
  673.4 23.0 %gather_fusion.1 = s32[4096]{0:T(1024)S(1)} fusion(s32[4096]{0:T(1024)S(1)} %get-tuple-element.417, u32[4096]{0:T(1024)S(1)} %broadcast_clamp_fusion.9), kind=kCustom, calls=%fused_computation.3.clone.clone.1 | custom fusion | bytes 49152 | tf_op jit(solution)/shard_map/jit(searchsorted)/jit(_searchsorted_scan_impl)/vmap(jit(_searchsorted_scan_impl))/while/body/eval_jaxpr/gather | solution.py:75
  696.5 15.5 %scatter_custom_fusion.2 = s32[4096]{0:T(1024)S(1)} fusion(s32[4096]{0:T(1024)S(1)} %get-tuple-element.335, s32[4096]{0:T(1024)S(1)} %convert_subtract_fusion, s32[]{:T(128)} %constant.249.clone.1), kind=kCustom, calls=%fused_computation.369 | custom fusion | bytes 16388 | tf_op jit(solution)/shard_map/scatter | solution.py:77
  712.1 15.5 %scatter_custom_fusion.3 = s32[4608]{0:T(1024)S(1)} fusion(s32[4096]{0:T(1024)S(1)} %get-tuple-element.323, s32[4096]{0:T(1024)S(1)} %get-tuple-element.332, s32[]{:T(128)} %constant.249.clone.1), kind=kCustom, calls=%fused_computation.360 | custom fusion | bytes 18436 | tf_op jit(solution)/shard_map/scatter | solution.py:108
  728.2 3.0 copy.55
  734.9 5.1 all-to-all-start.2
  740.1 5.5 all-to-all-done.2
  745.7 9.3 gather_fusion.4
  755.0 5.0 broadcast_select_fusion.1
  760.0 3.8 all-to-all-start.1
  764.1 2.8 copy.56
  766.9 49.0 %all-to-all-done.1 = f32[4,1,1152,128]{3,2,1,0:T(8,128)S(1)} async-done(((f32[4,1,1152,128]{3,2,1,0:T(8,128)}), f32[4,1,1152,128]{3,2,1,0:T(8,128)S(1)}, u32[]{:S(2)}, u32[]{:S(2)}) %all-to-all-start.1) | async-done | bytes 2359328 | tf_op jit(solution)/shard_map/all_to_all | solution.py:121
  815.8 14.1 %gather_fusion.5 = f32[4096,128]{1,0:T(8,128)} fusion(f32[4608,128]{1,0:T(8,128)S(1)} %bitcast.75, s32[4096]{0:T(1024)S(1)} %broadcast_clamp_fusion.3), kind=kCustom, calls=%fused_computation.2.clone | custom fusion | bytes 4210688 | tf_op jit(solution)/shard_map/jit(_take)/gather | solution.py:122
  830.0 1.9 copy.52
  837.5 2.9 copy.51
  842.1 9.3 gather_fusion.6
  851.5 5.0 broadcast_select_fusion
  856.4 3.9 all-to-all-start.3
  865.3 48.1 %all-to-all-done.3 = f32[4,1,1152,128]{3,2,1,0:T(8,128)S(1)} async-done(((f32[4,1,1152,128]{3,2,1,0:T(8,128)}), f32[4,1,1152,128]{3,2,1,0:T(8,128)S(1)}, u32[]{:S(2)}, u32[]{:S(2)}) %all-to-all-start.3) | async-done | bytes 2359328 | tf_op jit(solution)/shard_map/all_to_all | solution.py:121
  913.4 14.1 %gather_fusion.7 = f32[4096,128]{1,0:T(8,128)} fusion(f32[4608,128]{1,0:T(8,128)S(1)} %bitcast.74, s32[4096]{0:T(1024)S(1)} %broadcast_clamp_fusion.2), kind=kCustom, calls=%fused_computation.5.clone | custom fusion | bytes 4210688 | tf_op jit(solution)/shard_map/jit(_take)/gather | solution.py:122
  927.5 3.6 fusion
  931.1 1.9 slice.719
  934.9 1.9 slice.720
  936.8 2.0 copy.45
  942.6 2.8 copy.60
  946.0 3.2 fusion.7
  955.5 4.1 collective-permute-done.1
  961.2 2.1 copy.47
  966.1 4.8 collective-permute-start.3
  973.5 2.1 copy.50
  975.6 7.9 fusion.4
  (248 shorter events, 42.6 us)
Async XLA Ops:
  29.6 337.3 %copy-start.13 = (s32[8,512]{1,0:T(8,128)S(1)}, s32[8,512]{1,0:T(8,128)}, u32[]{:S(2)}) copy-start(s32[8,512]{1,0:T(8,128)} %param.24) | copy-start | bytes 49156
  362.0 372.8 %all-to-all-start = ((s32[4,1,1152]{2,1,0:T(1,128)}), s32[4,1,1152]{2,1,0:T(1,128)S(1)}, u32[]{:S(2)}, u32[]{:S(2)}) async-start(s32[4,1,1152]{2,1,0:T(1,128)} %reshape.190), calls=%async_computation | async-start | bytes 36864 | tf_op jit(solution)/shard_map/all_to_all | solution.py:110
  734.9 10.7 %all-to-all-start.2 = ((s32[4,1,1152]{2,1,0:T(1,128)}), s32[4,1,1152]{2,1,0:T(1,128)S(1)}, u32[]{:S(2)}, u32[]{:S(2)}) async-start(s32[4,1,1152]{2,1,0:T(1,128)} %reshape.195), calls=%async_computation.2 | async-start | bytes 36864 | tf_op jit(solution)/shard_map/all_to_all | solution.py:110
  760.0 3.8 copy-start.7
  760.0 55.8 %all-to-all-start.1 = ((f32[4,1,1152,128]{3,2,1,0:T(8,128)}), f32[4,1,1152,128]{3,2,1,0:T(8,128)S(1)}, u32[]{:S(2)}, u32[]{:S(2)}) async-start(f32[4,1,1152,128]{3,2,1,0:T(8,128)} %bitcast.77), calls=%async_computation.1 | async-start | bytes 4718592 | tf_op jit(solution)/shard_map/all_to_all | solution.py:121
  834.3 1.5 copy-start.5
  856.4 57.0 %all-to-all-start.3 = ((f32[4,1,1152,128]{3,2,1,0:T(8,128)}), f32[4,1,1152,128]{3,2,1,0:T(8,128)S(1)}, u32[]{:S(2)}, u32[]{:S(2)}) async-start(f32[4,1,1152,128]{3,2,1,0:T(8,128)} %bitcast.76), calls=%async_computation.3 | async-start | bytes 4718592 | tf_op jit(solution)/shard_map/all_to_all | solution.py:121
  862.4 1.9 copy-start
  862.4 1.9 copy-start.8
  940.3 2.2 copy-start.6
  942.6 2.8 copy-start.4
  946.0 6.7 copy-start.1
  946.0 6.7 copy-start.11
  949.1 12.1 %copy-start.2 = (f32[40,3,8,512]{3,2,1,0:T(8,128)}, f32[40,3,8,512]{3,2,1,0:T(8,128)S(1)}, u32[]{:S(2)}) copy-start(f32[40,3,8,512]{3,2,1,0:T(8,128)S(1)} %fusion.7) | copy-start | bytes 5898244
  949.5 6.0 collective-permute-start
  950.8 8.9 collective-permute-start.1
  952.6 2.9 copy-start.14
  963.3 8.9 collective-permute-start.2
  966.1 7.3 collective-permute-start.3
  975.6 7.9 copy-start.12
  975.6 8.0 copy-start.3
  975.6 8.0 copy-start.15
  983.7 0.8 copy-start.9
  983.7 0.8 copy-start.10
  985.7 1.3 copy-start.16
where the time goes:
time: 990 us; the launch traced here: 988 us
  local copies, waits for them, and re-layouts  801 us (81%)
  waiting for transfers between devices  108 us (11%)
  other arithmetic  49.4 us (5%)
  starting transfers between devices  26.9 us (3%)
    gather x26, local copies, waits for them, and re-layouts, slot_position(): first = jnp.searchsorted(sorted_partner, sorted_partner, side='left')  599 us
    all_to_all x2, waiting for transfers between devices, fetch(): lax.all_to_all(picked, 'across', split_axis=0, concat_axis=0, tiled=True)  97.1 us
    gather x2, local copies, waits for them, and re-layouts, slot_position(): sorted_partner = partner[order]  46 us
    scatter x2, local copies, waits for them, and re-layouts, fetch(): jnp.zeros((across_count * span * capacity,), jnp.int32).at[target]  31.1 us
    scatter x2, local copies, waits for them, and re-layouts, slot_position(): return jnp.zeros_like(partner).at[order].set(ranked)  31.1 us
    gather x2, local copies, waits for them, and re-layouts, fetch(): return jnp.take(returned.reshape(-1, width), target, axis=0)  28.2 us
    unnamed x66, local copies, waits for them, and re-layouts  23.1 us
  transfers between devices with their start and end apart: 8, of which 5 were waited for; matrix products, arithmetic and copies ran while one was open for 39% of the time, Pallas kernels for 0%

commit v1 on v0

--- a/solution.py
+++ b/solution.py
@@ -1,6 +1,10 @@
+import functools
+
 import jax
 import jax.numpy as jnp
 from jax import lax
+from jax.experimental import pallas as pl
+from jax.experimental.pallas import tpu as pltpu
 from jax.sharding import PartitionSpec as P
 
 
@@ -21,12 +25,6 @@
         after = lax.ppermute(first, axis, down)
         value = jnp.concatenate([before, value, after], axis=dim)
     return value
-
-
-def interpolate(columns, fraction):
-    upper = jnp.concatenate([columns[1:], columns[-1:]], axis=0)
-    weight = fraction[:, None]
-    return (1.0 - weight) * columns + weight * upper
 
 
 def neighbour_sum(padded):
@@ -69,12 +67,45 @@
     return (global_column // along_dev, global_row // cross_dev, local_cell)
 
 
-def slot_position(partner):
-    order = jnp.argsort(partner, stable=True)
-    sorted_partner = partner[order]
-    first = jnp.searchsorted(sorted_partner, sorted_partner, side="left")
-    ranked = jnp.arange(partner.shape[0], dtype=jnp.int32) - first
-    return jnp.zeros_like(partner).at[order].set(ranked)
+def prefix_count(member):
+    partners, cells = member.shape
+    lanes = 128
+    blocks = member.reshape(partners, cells // lanes, lanes)
+    before = jnp.triu(jnp.ones((lanes, lanes), jnp.bfloat16), 1)
+    inside = lax.dot_general(
+        blocks.astype(jnp.bfloat16), before, (((2,), (0,)), ((), ())),
+        preferred_element_type=jnp.float32,
+    ).astype(jnp.int32)
+    totals = blocks.sum(axis=2)
+    ahead = jnp.cumsum(totals, axis=1) - totals
+    return (inside + ahead[:, :, None]).reshape(partners, cells), totals.sum(axis=1)
+
+
+def plan(feet, cross_dev, along_dev):
+    along_count = lax.axis_size("along")
+    across_count = lax.axis_size("across")
+    cells = cross_dev * along_dev
+    reach = along_count // 8
+    capacity = 9 * cells // (8 * across_count * reach)
+    span = 2 * reach - 1
+    partners = across_count * span
+    owner_along, owner_across, local_cell = owners(
+        feet, cross_dev, along_dev, along_dev * along_count
+    )
+    offset = owner_along - lax.axis_index("along")
+    partner = owner_across * span + offset + reach - 1
+    member = (partner[None, :] == jnp.arange(partners, dtype=jnp.int32)[:, None]).astype(jnp.int32)
+    rank, counts = prefix_count(member)
+    target = jnp.sum(
+        member * (rank + capacity * jnp.arange(partners, dtype=jnp.int32)[:, None]), axis=0
+    )
+    key = (partner * cells + jnp.arange(cells, dtype=jnp.int32)) * cells + local_cell
+    ordered = jnp.pad(lax.sort(key) % cells, (0, capacity))
+    starts = jnp.cumsum(counts) - counts
+    requests = jnp.stack(
+        [lax.dynamic_slice(ordered, (starts[p],), (capacity,)) for p in range(partners)]
+    )
+    return requests.reshape(across_count, span, capacity), target
 
 
 def hop_groups(reach, power):
@@ -83,43 +114,82 @@
     return (upward, downward)
 
 
-def request_hop(message, steps):
-    return shifted(message, "along", steps)
-
-
-def column_hop(message, steps):
-    return shifted(message, "along", steps)
-
-
-def fetch(table, feet, cross_dev, along_dev):
-    along_count = lax.axis_size("along")
-    across_count = lax.axis_size("across")
-    reach = along_count // 8
-    capacity = 9 * cross_dev * along_dev // (8 * across_count * reach)
-    width = table.shape[1]
-    owner_along, owner_across, local_cell = owners(
-        feet, cross_dev, along_dev, along_dev * along_count
-    )
-    partner = owner_along * across_count + owner_across
-    position = slot_position(partner)
-    span = 2 * reach - 1
-    offset = owner_along - lax.axis_index("along")
-    target = (owner_across * span + offset + reach - 1) * capacity + position
-    requests = jnp.zeros((across_count * span * capacity,), jnp.int32).at[target].set(local_cell)
-    requests = requests.reshape(across_count, span, capacity)
+UNROLL = 32
+
+
+def gather_kernel(index_ref, table_ref, out_ref):
+    def step(i, carry):
+        base = pl.multiple_of(i * UNROLL, UNROLL)
+        for u in range(UNROLL):
+            out_ref[pl.ds(base + u, 1), :] = table_ref[pl.ds(index_ref[base + u], 1), :]
+        return carry
+
+    lax.fori_loop(0, out_ref.shape[0] // UNROLL, step, 0)
+
+
+def gather_rows(table, index):
+    count, width = index.shape[0], table.shape[1]
+    return pl.pallas_call(
+        gather_kernel,
+        out_shape=jax.ShapeDtypeStruct((count, width), table.dtype),
+        in_specs=[
+            pl.BlockSpec(memory_space=pltpu.SMEM),
+            pl.BlockSpec(memory_space=pltpu.VMEM),
+        ],
+        out_specs=pl.BlockSpec(memory_space=pltpu.VMEM),
+        name="gather_rows",
+    )(index, table)
+
+
+def blend_kernel(layers, index_ref, table_ref, fraction_ref, out_ref):
+    width = out_ref.shape[1]
+    lane = lax.broadcasted_iota(jnp.int32, (UNROLL, width), 1)
+    top = lane % layers == layers - 1
+
+    def step(i, carry):
+        base = pl.multiple_of(i * UNROLL, UNROLL)
+        for u in range(UNROLL):
+            out_ref[pl.ds(base + u, 1), :] = table_ref[pl.ds(index_ref[base + u], 1), :]
+        rows = out_ref[pl.ds(base, UNROLL), :]
+        upper = jnp.where(top, rows, pltpu.roll(rows, width - 1, 1))
+        weight = fraction_ref[pl.ds(base, UNROLL), :]
+        out_ref[pl.ds(base, UNROLL), :] = (1.0 - weight) * rows + weight * upper
+        return carry
+
+    lax.fori_loop(0, out_ref.shape[0] // UNROLL, step, 0)
+
+
+def blend_rows(table, index, fraction, layers):
+    return pl.pallas_call(
+        functools.partial(blend_kernel, layers),
+        out_shape=jax.ShapeDtypeStruct(fraction.shape, table.dtype),
+        in_specs=[
+            pl.BlockSpec(memory_space=pltpu.SMEM),
+            pl.BlockSpec(memory_space=pltpu.VMEM),
+            pl.BlockSpec(memory_space=pltpu.VMEM),
+        ],
+        out_specs=pl.BlockSpec(memory_space=pltpu.VMEM),
+        name="blend_rows",
+    )(index, table, fraction)
+
+
+def to_holders(requests):
+    reach = (requests.shape[1] + 1) // 2
     moved = lax.all_to_all(requests, "across", split_axis=0, concat_axis=0, tiled=True)
-    bit_count = (reach - 1).bit_length()
-    for power in range(bit_count):
+    for power in range((reach - 1).bit_length()):
         upward, downward = hop_groups(reach, power)
-        moved = moved.at[:, upward].set(request_hop(moved[:, upward], -(1 << power)))
-        moved = moved.at[:, downward].set(request_hop(moved[:, downward], 1 << power))
-    picked = jnp.take(table, moved.reshape(-1), axis=0).reshape(across_count, span, capacity, width)
-    for power in range(bit_count):
+        moved = moved.at[:, upward].set(shifted(moved[:, upward], "along", -(1 << power)))
+        moved = moved.at[:, downward].set(shifted(moved[:, downward], "along", 1 << power))
+    return moved
+
+
+def to_askers(picked):
+    reach = (picked.shape[1] + 1) // 2
+    for power in range((reach - 1).bit_length()):
         upward, downward = hop_groups(reach, power)
-        picked = picked.at[:, upward].set(column_hop(picked[:, upward], 1 << power))
-        picked = picked.at[:, downward].set(column_hop(picked[:, downward], -(1 << power)))
-    returned = lax.all_to_all(picked, "across", split_axis=0, concat_axis=0, tiled=True)
-    return jnp.take(returned.reshape(-1, width), target, axis=0)
+        picked = picked.at[:, upward].set(shifted(picked[:, upward], "along", 1 << power))
+        picked = picked.at[:, downward].set(shifted(picked[:, downward], "along", -(1 << power)))
+    return lax.all_to_all(picked, "across", split_axis=0, concat_axis=0, tiled=True)
 
 
 def body(
@@ -134,17 +204,30 @@
     surface_stress,
 ):
     layers, components, cross_dev, along_dev = fields.shape
+    cells = cross_dev * along_dev
     row_count = layers * components
     width = (row_count + 127) // 128 * 128
 
-    def advect(current, feet, fraction):
-        table = current.reshape(row_count, cross_dev * along_dev).T
-        table = jnp.pad(table, ((0, 0), (0, width - row_count)))
-        gathered = fetch(table, feet, cross_dev, along_dev)[:, :row_count].T
-        return interpolate(gathered.reshape(layers, components, cross_dev, along_dev), fraction)
-
-    middle = advect(fields, first_feet, first_fraction)
-    moved = advect(middle, second_feet, second_fraction)
+    first_requests, first_target = plan(first_feet, cross_dev, along_dev)
+    second_requests, second_target = plan(second_feet, cross_dev, along_dev)
+    capacity = first_requests.shape[2]
+    asked = to_holders(jnp.concatenate([first_requests, second_requests], axis=2))
+
+    def advect(table, asked, target, fraction):
+        weight = jnp.pad(
+            jnp.tile(fraction.reshape(layers, cells), (components, 1)),
+            ((0, width - row_count), (0, 0)),
+        ).T
+        picked = gather_rows(table, asked.reshape(-1))
+        returned = to_askers(picked.reshape(asked.shape + (width,)))
+        return blend_rows(returned.reshape(-1, width), target, weight, layers)
+
+    table = fields.transpose(1, 0, 2, 3).reshape(row_count, cells)
+    table = jnp.pad(table, ((0, width - row_count), (0, 0))).T
+    middle = advect(table, asked[:, :, :capacity], first_target, first_fraction)
+    moved = advect(middle, asked[:, :, capacity:], second_target, second_fraction)
+    moved = moved.T[:row_count].reshape(components, layers, cross_dev, along_dev)
+    moved = moved.transpose(1, 0, 2, 3)
     padded = padded_2(moved, (("across", 2), ("along", 3)), 1)
     beside_all = neighbour_sum(padded)
     row_total = cross_dev * lax.axis_size("across")

time: 990 us -> 258 us (0.26)
  local copies, waits for them, and re-layouts: 801 us -> 42.1 us
  Pallas kernels: 0 us -> 48.9 us
  other arithmetic: 49.4 us -> 29.5 us
  between operations: 0.82 us -> 15.6 us
  waiting for transfers between devices: 108 us -> 94.2 us
    gather x32 -> x0, local copies, waits for them, and re-layouts: 692 us -> none  [the longest x26 599 us: slot_position(): first = jnp.searchsorted(sorted_partner, sorted_partner, side='left')]
    scatter x4 -> x0, local copies, waits for them, and re-layouts: 62.1 us -> none  [the longest x2 31.1 us: fetch(): jnp.zeros((across_count * span * capacity,), jnp.int32).at[target]]
    pallas_call x0 -> x4, Pallas kernels: none -> 48.9 us  [the longest x2 34.2 us: blend_rows(): pl.pallas_call(functools.partial(blend_kernel, layers), out_shape=jax.Sha...]
    all_to_all x4 -> x3, waiting for transfers between devices: 103 us -> 88.9 us  [the longest x2 88.9 us: to_askers(): lax.all_to_all(picked, 'across', split_axis=0, concat_axis=0, tiled=True)]
    unnamed x66 -> x51, local copies, waits for them, and re-layouts: 23.1 us -> 10.5 us
    select_n x56 -> x2, other arithmetic: 10.6 us -> 0.02 us  [plan(): ordered = jnp.pad(lax.sort(key) % cells, (0, capacity))]
  transfers between devices with their start and end apart: 8 -> 7, of which waited for: 5 -> 4; matrix products, arithmetic and copies ran while one was open for 39% -> 12% of each run, Pallas kernels for 0% -> 0%
where the time goes in v1:
time: 258 us; the launch traced here: 256 us
  waiting for transfers between devices  94.2 us (37%)
  Pallas kernels  48.9 us (19%)
  local copies, waits for them, and re-layouts  42.1 us (16%)
  other arithmetic  29.5 us (11%)
  starting transfers between devices  23.9 us (9%)
  between operations  15.6 us (6%)
    all_to_all x2, waiting for transfers between devices, to_askers(): lax.all_to_all(picked, 'across', split_axis=0, concat_axis=0, tiled=True)  88.9 us
    pallas_call x2, Pallas kernels, blend_rows(): pl.pallas_call(functools.partial(blend_kernel, layers), out_shape=jax.Sha...  34.2 us
    pallas_call x2, Pallas kernels, gather_rows(): pl.pallas_call(gather_kernel, out_shape=jax.ShapeDtypeStruct((count, widt...  14.6 us
    sort x2, other arithmetic, plan(): ordered = jnp.pad(lax.sort(key) % cells, (0, capacity))  11.6 us
    unnamed x51, local copies, waits for them, and re-layouts  10.5 us
    all_to_all x2, starting transfers between devices, to_askers(): lax.all_to_all(picked, 'across', split_axis=0, concat_axis=0, tiled=True)  10 us
    add x1, other arithmetic, body(): mixed = moved + lateral_mix * (beside_all - present * moved)  6.66 us
    another operation x4, local copies, waits for them, and re-layouts, advect(): jnp.tile(fraction.reshape(layers, cells), (components, 1))  6.42 us
  transfers between devices with their start and end apart: 7, of which 4 were waited for; matrix products, arithmetic and copies ran while one was open for 12% of the time, Pallas kernels for 0%

profile of v1, /device:TPU:4, one launch (start us, length us, event | category | flops | bytes accessed | tf_op | source)
XLA Modules:
  0.0 255.7 jit_solution(2404737876323138373)
XLA Ops:
  0.0 0.7 reshape.459
  0.7 0.7 reshape.461
  1.5 0.2 convert_reduce_fusion
  1.9 0.7 fusion.163
  7.6 0.2 convert_reduce_fusion.2
  8.0 0.7 fusion.164
  13.7 0.7 copy.32
  14.4 0.7 copy.33
  15.2 5.8 %sort.28 = (s32[4096]{0:T(1024)S(1)}, s32[4096]{0:T(1024)}) sort(s32[4096]{0:T(1024)S(1)} %get-tuple-element.162, s32[4096]{0:T(1024)S(1)} %iota.75), dimensions={0}, to_apply=%region_3.4 | sort | flops 49152 | bytes 65536 | tf_op jit(solution)/shard_map/sort | solution.py:103
  23.7 5.8 %sort.29 = (s32[4096]{0:T(1024)S(1)}, s32[4096]{0:T(1024)}) sort(s32[4096]{0:T(1024)S(1)} %get-tuple-element.163, s32[4096]{0:T(1024)S(1)} %iota.77), dimensions={0}, to_apply=%region_6.7 | sort | flops 49152 | bytes 65536 | tf_op jit(solution)/shard_map/sort | solution.py:103
  32.2 0.6 pad_add_fusion.1
  32.8 4.9 %all-to-all-start = ((s32[4,1,2304]{2,1,0:T(1,128)}), s32[4,1,2304]{2,1,0:T(1,128)S(1)}, u32[]{:S(2)}, u32[]{:S(2)}) async-start(s32[4,1,2304]{2,1,0:T(1,128)} %pad_add_fusion.1), calls=%async_computation | async-start | bytes 73728 | tf_op jit(solution)/shard_map/all_to_all | solution.py:178
  37.7 1.7 copy.20
  39.4 2.8 %copy.34 = f32[15,8,8,512]{3,1,2,0:T(8,128)} copy(f32[15,8,8,512]{3,2,1,0:T(8,128)S(1)} %bitcast.92) | data formatting | bytes 3932160
  42.2 1.9 copy.21
  44.1 1.5 pad_bitcast_fusion.2.table_ref
  45.6 0.6 reshape.470.index_ref
  46.3 7.3 %gather_rows.2 = f32[4608,128]{1,0:T(8,128)} custom-call(s32[4608]{0:T(1024)} %reshape.470.index_ref, f32[4096,128]{1,0:T(8,128)} %pad_bitcast_fusion.2.table_ref), custom_call_target="tpu_custom_call" | custom-call | tf_op jit(solution)/shard_map/gather_rows/pallas_call | solution.py:132
  53.6 5.2 %all-to-all-start.1 = ((f32[4,1,1152,128]{3,2,1,0:T(8,128)}), f32[4,1,1152,128]{3,2,1,0:T(8,128)S(1)}, u32[]{:S(2)}, u32[]{:S(2)}) async-start(f32[4,1,1152,128]{3,2,1,0:T(8,128)} %bitcast.85), calls=%async_computation.1 | async-start | bytes 4718592 | tf_op jit(solution)/shard_map/all_to_all | solution.py:192
  58.8 0.2 reduce_window_sum.27
  59.0 0.4 copy.35
  59.4 1.5 tile.21
  60.9 2.9 %copy.23 = f32[120,4096]{0,1:T(8,128)} copy(f32[120,4096]{1,0:T(8,128)} %bitcast.88) | data formatting | bytes 3932160 | tf_op jit(solution)/shard_map/tile | solution.py:218
  63.8 0.7 fusion.13
  64.5 3.0 %pad_bitcast_fusion.1.fraction_ref = f32[4096,128]{1,0:T(8,128)} fusion(f32[120,4096]{0,1:T(8,128)} %copy.23), kind=kLoop, calls=%fused_computation.1 | loop fusion | bytes 4063232 | tf_op jit(solution)/shard_map/transpose | solution.py:220
  67.6 0.6 reshape.469.index_ref
  68.2 43.9 %all-to-all-done.1 = f32[4,1,1152,128]{3,2,1,0:T(8,128)S(1)} async-done(((f32[4,1,1152,128]{3,2,1,0:T(8,128)}), f32[4,1,1152,128]{3,2,1,0:T(8,128)S(1)}, u32[]{:S(2)}, u32[]{:S(2)}) %all-to-all-start.1) | async-done | bytes 2359328 | tf_op jit(solution)/shard_map/all_to_all | solution.py:192
  112.1 1.4 copy-done.1
  113.5 17.2 %blend_rows.2.table_ref = f32[4096,128]{1,0:T(8,128)} custom-call(s32[4096]{0:T(1024)} %bitcast.106, f32[4608,128]{1,0:T(8,128)} %bitcast.83, f32[4096,128]{1,0:T(8,128)} %pad_bitcast_fusion.1.fraction_ref), custom_call_target="tpu_custom_call" | custom-call | tf_op jit(solution)/shard_map/blend_rows/pallas_call | solution.py:163
  130.6 7.3 %gather_rows.3 = f32[4608,128]{1,0:T(8,128)} custom-call(s32[4608]{0:T(1024)} %reshape.469.index_ref, f32[4096,128]{1,0:T(8,128)} %blend_rows.2.table_ref), custom_call_target="tpu_custom_call" | custom-call | tf_op jit(solution)/shard_map/gather_rows/pallas_call | solution.py:132
  138.0 4.8 %all-to-all-start.2 = ((f32[4,1,1152,128]{3,2,1,0:T(8,128)}), f32[4,1,1152,128]{3,2,1,0:T(8,128)}, u32[]{:S(2)}, u32[]{:S(2)}) async-start(f32[4,1,1152,128]{3,2,1,0:T(8,128)} %bitcast.84), calls=%async_computation.2 | async-start | bytes 4718592 | tf_op jit(solution)/shard_map/all_to_all | solution.py:192
  142.8 0.2 reduce_window_sum.26
  143.0 0.4 copy.36
  143.4 0.2 tile.24
  143.6 1.9 copy.25
  145.4 0.6 convert_add_fusion
  146.0 0.7 fusion.12
  146.9 0.3 pad_maximum_fusion.8
  147.1 1.6 pad_add_fusion
  148.7 0.7 copy-done.3
  149.4 1.5 pad_bitcast_fusion.fraction_ref
  150.9 45.1 %all-to-all-done.2 = f32[4,1,1152,128]{3,2,1,0:T(8,128)} async-done(((f32[4,1,1152,128]{3,2,1,0:T(8,128)}), f32[4,1,1152,128]{3,2,1,0:T(8,128)}, u32[]{:S(2)}, u32[]{:S(2)}) %all-to-all-start.2) | async-done | bytes 2359328 | tf_op jit(solution)/shard_map/all_to_all | solution.py:192
  196.0 17.1 %blend_rows.3 = f32[4096,128]{1,0:T(8,128)} custom-call(s32[4096]{0:T(1024)} %bitcast.105, f32[4608,128]{1,0:T(8,128)} %bitcast.24.table_ref, f32[4096,128]{1,0:T(8,128)} %pad_bitcast_fusion.fraction_ref), custom_call_target="tpu_custom_call" | custom-call | tf_op jit(solution)/shard_map/blend_rows/pallas_call | solution.py:163
  213.1 2.9 %copy.26 = f32[120,4096]{1,0:T(8,128)} copy(f32[120,4096]{0,1:T(8,128)} %bitcast.86) | data formatting | bytes 3932160 | tf_op jit(solution)/shard_map/slice | solution.py:229
  216.0 3.0 %copy.37 = f32[15,8,8,512]{3,2,1,0:T(8,128)S(1)} copy(f32[15,8,8,512]{3,1,2,0:T(8,128)} %bitcast.90) | data formatting | bytes 3932160
  219.2 0.3 fusion.162
  219.5 1.3 collective-permute-start
  220.8 1.3 collective-permute-start.1
  222.1 0.6 fusion.120
  222.8 1.7 slice_subtract_fusion.34
  224.5 1.1 collective-permute-done
  225.6 4.1 %collective-permute-done.1 = f32[40,3,1,512]{3,2,0,1:T(1,128)S(1)} collective-permute-done((f32[40,3,1,512]{3,2,0,1:T(1,128)S(1)}, f32[40,3,1,512]{3,2,0,1:T(1,128)S(1)}, u32[]{:S(2)}, u32[]{:S(2)}) %collective-permute-start.1) | collective-permute-done | bytes 245792 | tf_op jit(solution)/shard_map/ppermute | solution.py:25
  229.7 1.6 pad_maximum_fusion.11
  231.3 2.1 copy.27
  233.4 1.9 collective-permute-start.2
  235.3 0.9 copy.29
  236.2 4.5 %collective-permute-start.3 = (f32[40,3,10,1]{0,3,2,1:T(1,128)}, f32[40,3,10,1]{0,3,2,1:T(1,128)}, u32[]{:S(2)}, u32[]{:S(2)}) collective-permute-start(f32[40,3,10,1]{0,3,2,1:T(1,128)} %copy.29), channel_id=1, source_target_pairs={{4,0},{8,4},{12,8},{16,12},{20,16},{24,20},{28,24},{5,1},{9,5},{13... | collective-permute-start | bytes 14408 | tf_op jit(solution)/shard_map/ppermute | solution.py:25
  240.8 1.4 broadcast_add_fusion
  242.1 1.2 copy.28
  243.4 2.1 copy.30
  245.5 6.7 %fusion.3 = f32[40,3,8,512]{3,2,0,1:T(8,128)S(1)} fusion(f32[40,3,8,512]{3,2,0,1:T(8,128)} %copy-done, f32[40,3,10,1]{3,2,0,1:T(8,128)} %copy.30, f32[40,3,1,512]{3,2,0,1:T(1,128)S(1)} %collective-permute-done.1, f32[40,3,1,512]{3,2,0,1:T(1,128)S(1)} %collective-permute-done, f32[40,3,10,1]{3,2,0,1:T(8,128)S(1)} %copy.28, f32[8,512]{1,0:T(8,128)} %broadcast_add_fusion, ...), kind=kLoop, calls=%fused_computation.8 | loop fusion | flops 7372800 | bytes 4466048 | tf_op jit(solution)/shard_map/add | solution.py:244
  252.3 0.7 fusion.17
  253.1 0.5 constant_dynamic-update-slice_fusion.39
  254.3 1.4 copy.31
  (99 shorter events, 2.0 us)
Async XLA Ops:
  32.8 12.7 %all-to-all-start = ((s32[4,1,2304]{2,1,0:T(1,128)}), s32[4,1,2304]{2,1,0:T(1,128)S(1)}, u32[]{:S(2)}, u32[]{:S(2)}) async-start(s32[4,1,2304]{2,1,0:T(1,128)} %pad_add_fusion.1), calls=%async_computation | async-start | bytes 73728 | tf_op jit(solution)/shard_map/all_to_all | solution.py:178
  53.6 5.4 %copy-start.5 = (f32[40,8,512]{2,1,0:T(8,128)S(1)}, f32[40,8,512]{2,1,0:T(8,128)}, u32[]{:S(2)}) copy-start(f32[40,8,512]{2,1,0:T(8,128)} %param.15) | copy-start | bytes 1966084
  53.6 58.5 %all-to-all-start.1 = ((f32[4,1,1152,128]{3,2,1,0:T(8,128)}), f32[4,1,1152,128]{3,2,1,0:T(8,128)S(1)}, u32[]{:S(2)}, u32[]{:S(2)}) async-start(f32[4,1,1152,128]{3,2,1,0:T(8,128)} %bitcast.85), calls=%async_computation.1 | async-start | bytes 4718592 | tf_op jit(solution)/shard_map/all_to_all | solution.py:192
  112.1 1.4 copy-start.1
  138.0 5.0 %copy-start.6 = (f32[40,8,512]{2,1,0:T(8,128)S(1)}, f32[40,8,512]{2,1,0:T(8,128)}, u32[]{:S(2)}) copy-start(f32[40,8,512]{2,1,0:T(8,128)} %param.17) | copy-start | bytes 1966084
  138.0 58.1 %all-to-all-start.2 = ((f32[4,1,1152,128]{3,2,1,0:T(8,128)}), f32[4,1,1152,128]{3,2,1,0:T(8,128)}, u32[]{:S(2)}, u32[]{:S(2)}) async-start(f32[4,1,1152,128]{3,2,1,0:T(8,128)} %bitcast.84), calls=%async_computation.2 | async-start | bytes 4718592 | tf_op jit(solution)/shard_map/all_to_all | solution.py:192
  143.6 3.2 %copy-start.4 = (f32[2,39,8,512]{3,2,1,0:T(8,128)S(1)}, f32[2,39,8,512]{3,2,1,0:T(8,128)}, u32[]{:S(2)}) copy-start(f32[2,39,8,512]{3,2,1,0:T(8,128)} %param.19) | copy-start | bytes 3833860
  147.1 2.3 copy-start.3
  219.0 3.8 %copy-start.9 = (f32[8,512]{1,0:T(8,128)S(1)}, f32[8,512]{1,0:T(8,128)}, u32[]{:S(2)}) copy-start(f32[8,512]{1,0:T(8,128)} %param.20) | copy-start | bytes 49156
  219.2 12.1 %copy-start = (f32[40,3,8,512]{3,2,0,1:T(8,128)}, f32[40,3,8,512]{3,2,0,1:T(8,128)S(1)}, u32[]{:S(2)}) copy-start(f32[40,3,8,512]{3,2,0,1:T(8,128)S(1)} %bitcast_bitcast_fusion) | copy-start | bytes 5898244
  219.5 6.1 %collective-permute-start = (f32[40,3,1,512]{3,2,0,1:T(1,128)S(1)}, f32[40,3,1,512]{3,2,0,1:T(1,128)S(1)}, u32[]{:S(2)}, u32[]{:S(2)}) collective-permute-start(f32[40,3,1,512]{3,2,0,1:T(1,128)S(1)} %get-tuple-element.140), channel_id=1, source_target_pairs={{0,1},{1,2},{2,3},{4,5},{5,6},{6,7},{8,9},{9,10},{10,11},{12,13},{... | collective-permute-start | bytes 737288 | tf_op jit(solution)/shard_map/ppermute | solution.py:24
  220.8 8.9 %collective-permute-start.1 = (f32[40,3,1,512]{3,2,0,1:T(1,128)S(1)}, f32[40,3,1,512]{3,2,0,1:T(1,128)S(1)}, u32[]{:S(2)}, u32[]{:S(2)}) collective-permute-start(f32[40,3,1,512]{3,2,0,1:T(1,128)S(1)} %get-tuple-element.141), channel_id=1, source_target_pairs={{1,0},{2,1},{3,2},{5,4},{6,5},{7,6},{9,8},{10,9},{11,10},{13,12},{... | collective-permute-start | bytes 737288 | tf_op jit(solution)/shard_map/ppermute | solution.py:25
  222.8 2.8 %copy-start.11 = (f32[3]{0:T(128)}, f32[3]{0:T(128)S(1)}, u32[]{:S(2)}) copy-start(f32[3]{0:T(128)S(1)} %pad.32.clone) | copy-start | bytes 40
  233.4 8.7 %collective-permute-start.2 = (f32[40,3,10,1]{0,3,2,1:T(1,128)}, f32[40,3,10,1]{0,3,2,1:T(1,128)}, u32[]{:S(2)}, u32[]{:S(2)}) collective-permute-start(f32[40,3,10,1]{0,3,2,1:T(1,128)} %copy.27), channel_id=1, source_target_pairs={{0,4},{4,8},{8,12},{12,16},{16,20},{20,24},{24,28},{1,5},{5,9},{9,... | collective-permute-start | bytes 14408 | tf_op jit(solution)/shard_map/ppermute | solution.py:24
  236.2 7.1 %collective-permute-start.3 = (f32[40,3,10,1]{0,3,2,1:T(1,128)}, f32[40,3,10,1]{0,3,2,1:T(1,128)}, u32[]{:S(2)}, u32[]{:S(2)}) collective-permute-start(f32[40,3,10,1]{0,3,2,1:T(1,128)} %copy.29), channel_id=1, source_target_pairs={{4,0},{8,4},{12,8},{16,12},{20,16},{24,20},{28,24},{5,1},{9,5},{13... | collective-permute-start | bytes 14408 | tf_op jit(solution)/shard_map/ppermute | solution.py:25
  245.5 6.7 %copy-start.10 = (f32[2,8,512]{2,1,0:T(8,128)S(1)}, f32[2,8,512]{2,1,0:T(8,128)}, u32[]{:S(2)}) copy-start(f32[2,8,512]{2,1,0:T(8,128)} %param.21) | copy-start | bytes 98308
  245.5 6.7 %copy-start.2 = (f32[40,3,8,512]{3,2,0,1:T(8,128)S(1)}, f32[40,3,8,512]{3,2,0,1:T(8,128)}, u32[]{:S(2)}) copy-start(f32[40,3,8,512]{3,2,0,1:T(8,128)} %pad_add_fusion) | copy-start | bytes 5898244
  245.5 6.7 %copy-start.12 = (f32[3]{0:T(128)S(1)}, f32[3]{0:T(128)}, u32[]{:S(2)}) copy-start(f32[3]{0:T(128)} %copy-done.11) | copy-start | bytes 40
  252.3 0.8 copy-start.7
  252.3 0.8 copy-start.8

commit v2 on v1

--- a/solution.py
+++ b/solution.py
@@ -60,7 +60,7 @@
 
 
 def owners(feet, cross_dev, along_dev, along_total):
-    flat_feet = feet.reshape(-1)
+    flat_feet = feet
     global_row = flat_feet // along_total
     global_column = flat_feet % along_total
     local_cell = global_row % cross_dev * along_dev + global_column % along_dev
@@ -89,23 +89,27 @@
     capacity = 9 * cells // (8 * across_count * reach)
     span = 2 * reach - 1
     partners = across_count * span
+    substeps = feet.shape[0]
     owner_along, owner_across, local_cell = owners(
-        feet, cross_dev, along_dev, along_dev * along_count
+        feet.reshape(substeps, cells), cross_dev, along_dev, along_dev * along_count
     )
     offset = owner_along - lax.axis_index("along")
     partner = owner_across * span + offset + reach - 1
-    member = (partner[None, :] == jnp.arange(partners, dtype=jnp.int32)[:, None]).astype(jnp.int32)
-    rank, counts = prefix_count(member)
-    target = jnp.sum(
-        member * (rank + capacity * jnp.arange(partners, dtype=jnp.int32)[:, None]), axis=0
-    )
     key = (partner * cells + jnp.arange(cells, dtype=jnp.int32)) * cells + local_cell
-    ordered = jnp.pad(lax.sort(key) % cells, (0, capacity))
-    starts = jnp.cumsum(counts) - counts
-    requests = jnp.stack(
-        [lax.dynamic_slice(ordered, (starts[p],), (capacity,)) for p in range(partners)]
-    )
-    return requests.reshape(across_count, span, capacity), target
+    ordered = jnp.pad(lax.sort(key, dimension=1) % cells, ((0, 0), (0, capacity)))
+    labels = jnp.arange(partners, dtype=jnp.int32)[:, None]
+    member = (partner[:, None, :] == labels).astype(jnp.int32)
+    rank, counts = prefix_count(member.reshape(substeps * partners, cells))
+    rank = rank.reshape(substeps, partners, cells)
+    target = jnp.sum(member * (rank + capacity * labels), axis=1)
+    counts = counts.reshape(substeps, partners)
+    starts = jnp.cumsum(counts, axis=1) - counts
+    requests = [
+        lax.dynamic_slice(ordered[s], (starts[s, p],), (capacity,))
+        for p in range(partners)
+        for s in range(substeps)
+    ]
+    return jnp.stack(requests).reshape(across_count, span, substeps, capacity), target
 
 
 def hop_groups(reach, power):
@@ -190,6 +194,281 @@
         picked = picked.at[:, upward].set(shifted(picked[:, upward], "along", 1 << power))
         picked = picked.at[:, downward].set(shifted(picked[:, downward], "along", -(1 << power)))
     return lax.all_to_all(picked, "across", split_axis=0, concat_axis=0, tiled=True)
+
+
+LANES = 128
+PIECES = 3
+MESH = pl.DeviceIdType.MESH
+
+
+def blend(rows, weight, top):
+    upper = jnp.where(top, rows, pltpu.roll(rows, rows.shape[1] - 1, 1))
+    return (1.0 - weight) * rows + weight * upper
+
+
+def exchange_kernel(
+    layers,
+    components,
+    cross_dev,
+    capacity,
+    target_ref,
+    requests_ref,
+    fields_hbm,
+    first_hbm,
+    second_hbm,
+    out_hbm,
+    fields_ref,
+    first_ref,
+    second_ref,
+    out_ref,
+    asked_vmem,
+    asked,
+    table,
+    first_rows,
+    second_rows,
+    sent_1,
+    sent_2,
+    back_1,
+    back_2,
+    stage,
+    stage_weight,
+    final,
+    ask_send,
+    ask_recv,
+    ask_local,
+    send_sem,
+    recv_sem,
+    load_sem,
+):
+    tiles = fields_ref.shape[0]
+    along_dev = tiles * LANES
+    cells = cross_dev * along_dev
+    width = table.shape[1]
+    blocks = capacity // LANES
+    piece = capacity // PIECES
+    along = lax.axis_index("along")
+    me = lax.axis_index("across")
+    peers = [lax.rem(me + 2, 4), 3 - me, me + 1 - 2 * lax.rem(me, 2)]
+    pad = jnp.zeros((width - layers * components, LANES), jnp.float32)
+    top = lax.broadcasted_iota(jnp.int32, (LANES, width), 1) % layers == layers - 1
+
+    loads = [
+        [
+            pltpu.make_async_copy(
+                source.at[:, pl.ds(t * LANES, LANES)], place.at[t], load_sem.at[s, t]
+            )
+            for t in range(tiles)
+        ]
+        for s, (source, place) in enumerate(
+            [(fields_hbm, fields_ref), (first_hbm, first_ref), (second_hbm, second_ref)]
+        )
+    ]
+    for group in loads:
+        for copy in group:
+            copy.start()
+
+    barrier = pltpu.get_barrier_semaphore()
+    for peer in peers:
+        pl.semaphore_signal(barrier, inc=1, device_id=(along, peer), device_id_type=MESH)
+    pl.semaphore_wait(barrier, 3)
+
+    asks = []
+    for j, peer in enumerate(peers):
+        copy = pltpu.make_async_remote_copy(
+            src_ref=requests_ref.at[peer],
+            dst_ref=asked_vmem.at[me],
+            send_sem=ask_send.at[j],
+            recv_sem=ask_recv.at[j],
+            device_id=(along, peer),
+            device_id_type=MESH,
+        )
+        copy.start()
+        asks.append(copy)
+    own = pltpu.make_async_copy(requests_ref.at[me], asked.at[me], ask_local.at[3])
+    own.start()
+
+    for copy in loads[0]:
+        copy.wait()
+
+    def fill_table(i, carry):
+        for t in range(tiles):
+            parts = [
+                fields_ref[t, pl.ds(m * cross_dev + i, layers, stride=components * cross_dev), :]
+                for m in range(components)
+            ]
+            rows = jnp.concatenate(parts + [pad], axis=0).T
+            table[pl.ds(pl.multiple_of(i * along_dev + t * LANES, LANES), LANES), :] = rows
+        return carry
+
+    lax.fori_loop(0, cross_dev, fill_table, 0)
+
+    def fill_weight(source, rows_ref):
+        def step(i, carry):
+            for t in range(tiles):
+                part = source[t, pl.ds(i, layers, stride=cross_dev), :]
+                rows = jnp.concatenate([part] * components + [pad], axis=0).T
+                rows_ref[pl.ds(pl.multiple_of(i * along_dev + t * LANES, LANES), LANES), :] = rows
+            return carry
+
+        lax.fori_loop(0, cross_dev, step, 0)
+
+    locals_ = []
+    for j, peer in enumerate(peers):
+        asks[j].wait_recv()
+        copy = pltpu.make_async_copy(asked_vmem.at[peer], asked.at[peer], ask_local.at[j])
+        copy.start()
+        locals_.append(copy)
+    for copy in locals_ + [own]:
+        copy.wait()
+
+    def gather_1(peer, c, dst, base):
+        def step(b, carry):
+            row = c * (piece // LANES) + b
+            start = pl.multiple_of(base + b * LANES, LANES)
+            for u in range(LANES):
+                dst[pl.ds(start + u, 1), :] = table[pl.ds(asked[peer, row, u], 1), :]
+            return carry
+
+        lax.fori_loop(0, piece // LANES, step, 0)
+
+    def gather_2(peer, c, dst, base):
+        def step(b, carry):
+            row = blocks + c * (piece // LANES) + b
+            start = pl.multiple_of(base + b * LANES, LANES)
+            for u in range(LANES):
+                cell = asked[peer, row, u]
+                stage[pl.ds(u, 1), :] = back_1[pl.ds(target_ref[0, cell], 1), :]
+                stage_weight[pl.ds(u, 1), :] = first_rows[pl.ds(cell, 1), :]
+            dst[pl.ds(start, LANES), :] = blend(stage[...], stage_weight[...], top)
+            return carry
+
+        lax.fori_loop(0, piece // LANES, step, 0)
+
+    def exchange(gather, phase, sent, back, beside):
+        copies = []
+        for c in range(PIECES):
+            for j, peer in enumerate(peers[:2]):
+                copies.append((j, peer, c))
+        for c in range(PIECES):
+            copies.append((2, peers[2], c))
+        started = []
+        waiting = None
+        for j, peer, c in copies:
+            base = j * capacity + c * piece
+            gather(peer, c, sent, base)
+            copy = pltpu.make_async_remote_copy(
+                src_ref=sent.at[pl.ds(base, piece)],
+                dst_ref=back.at[pl.ds(pl.multiple_of(me * capacity + c * piece, LANES), piece)],
+                send_sem=send_sem.at[phase, j, c],
+                recv_sem=recv_sem.at[phase, j, c],
+                device_id=(along, peer),
+                device_id_type=MESH,
+            )
+            if waiting is not None:
+                waiting.start()
+            waiting = copy
+            started.append(copy)
+        for c in range(PIECES):
+            gather(me, c, back, me * capacity + c * piece)
+            if waiting is not None:
+                waiting.start()
+                waiting = None
+        beside()
+        for copy in started:
+            copy.wait()
+
+    def weights():
+        for copy in loads[1] + loads[2]:
+            copy.wait()
+        fill_weight(first_ref, first_rows)
+        fill_weight(second_ref, second_rows)
+
+    exchange(gather_1, 0, sent_1, back_1, weights)
+    exchange(gather_2, 1, sent_2, back_2, lambda: None)
+
+    def last(b, carry):
+        start = pl.multiple_of(b * LANES, LANES)
+        for u in range(LANES):
+            final[pl.ds(start + u, 1), :] = back_2[pl.ds(target_ref[1, start + u], 1), :]
+        return carry
+
+    lax.fori_loop(0, cells // LANES, last, 0)
+
+    def emit(i, carry):
+        for t in range(tiles):
+            rows = pl.ds(pl.multiple_of(i * along_dev + t * LANES, LANES), LANES)
+            value = blend(final[rows, :], second_rows[rows, :], top).T
+            for m in range(components):
+                out_ref[
+                    t, pl.ds(m * cross_dev + i, layers, stride=components * cross_dev), :
+                ] = value[m * layers : (m + 1) * layers]
+        return carry
+
+    lax.fori_loop(0, cross_dev, emit, 0)
+    stores = [
+        pltpu.make_async_copy(
+            out_ref.at[t], out_hbm.at[:, pl.ds(t * LANES, LANES)], load_sem.at[3, t]
+        )
+        for t in range(tiles)
+    ]
+    for copy in stores:
+        copy.start()
+    for copy in stores:
+        copy.wait()
+    for copy in asks:
+        copy.wait_send()
+
+
+def advect_twice(fields, requests, target, first_fraction, second_fraction):
+    layers, components, cross_dev, along_dev = fields.shape
+    cells = cross_dev * along_dev
+    partners, substeps, capacity = requests.shape
+    width = (layers * components + LANES - 1) // LANES * LANES
+    vmem = pl.BlockSpec(memory_space=pltpu.VMEM)
+    smem = pl.BlockSpec(memory_space=pltpu.SMEM)
+    hbm = pl.BlockSpec(memory_space=pl.ANY)
+    tiles = along_dev // LANES
+    grid = requests.reshape(partners, substeps * capacity // LANES, LANES)
+    rows = lambda count: pltpu.VMEM((count, width), jnp.float32)
+    moved = pl.pallas_call(
+        functools.partial(exchange_kernel, layers, components, cross_dev, capacity),
+        out_shape=jax.ShapeDtypeStruct((layers * components * cross_dev, along_dev), jnp.float32),
+        in_specs=[smem, vmem, hbm, hbm, hbm],
+        out_specs=hbm,
+        scratch_shapes=[
+            pltpu.VMEM((tiles, layers * components * cross_dev, LANES), jnp.float32),
+            pltpu.VMEM((tiles, layers * cross_dev, LANES), jnp.float32),
+            pltpu.VMEM((tiles, layers * cross_dev, LANES), jnp.float32),
+            pltpu.VMEM((tiles, layers * components * cross_dev, LANES), jnp.float32),
+            pltpu.VMEM(grid.shape, jnp.int32),
+            pltpu.SMEM(grid.shape, jnp.int32),
+            rows(cells),
+            rows(cells),
+            rows(cells),
+            rows(3 * capacity),
+            rows(3 * capacity),
+            rows(4 * capacity),
+            rows(4 * capacity),
+            rows(LANES),
+            rows(LANES),
+            rows(cells),
+            pltpu.SemaphoreType.DMA((3,)),
+            pltpu.SemaphoreType.DMA((3,)),
+            pltpu.SemaphoreType.DMA((4,)),
+            pltpu.SemaphoreType.DMA((2, 3, PIECES)),
+            pltpu.SemaphoreType.DMA((2, 3, PIECES)),
+            pltpu.SemaphoreType.DMA((4, tiles)),
+        ],
+        compiler_params=pltpu.CompilerParams(collective_id=0, has_side_effects=True),
+        name="advect_twice",
+    )(
+        target,
+        grid,
+        fields.reshape(layers * components * cross_dev, along_dev),
+        first_fraction.reshape(layers * cross_dev, along_dev),
+        second_fraction.reshape(layers * cross_dev, along_dev),
+    )
+    return moved.reshape(fields.shape)
 
 
 def body(
@@ -208,26 +487,29 @@
     row_count = layers * components
     width = (row_count + 127) // 128 * 128
 
-    first_requests, first_target = plan(first_feet, cross_dev, along_dev)
-    second_requests, second_target = plan(second_feet, cross_dev, along_dev)
-    capacity = first_requests.shape[2]
-    asked = to_holders(jnp.concatenate([first_requests, second_requests], axis=2))
-
-    def advect(table, asked, target, fraction):
-        weight = jnp.pad(
-            jnp.tile(fraction.reshape(layers, cells), (components, 1)),
-            ((0, width - row_count), (0, 0)),
-        ).T
-        picked = gather_rows(table, asked.reshape(-1))
-        returned = to_askers(picked.reshape(asked.shape + (width,)))
-        return blend_rows(returned.reshape(-1, width), target, weight, layers)
-
-    table = fields.transpose(1, 0, 2, 3).reshape(row_count, cells)
-    table = jnp.pad(table, ((0, width - row_count), (0, 0))).T
-    middle = advect(table, asked[:, :, :capacity], first_target, first_fraction)
-    moved = advect(middle, asked[:, :, capacity:], second_target, second_fraction)
-    moved = moved.T[:row_count].reshape(components, layers, cross_dev, along_dev)
-    moved = moved.transpose(1, 0, 2, 3)
+    requests, target = plan(jnp.stack([first_feet, second_feet]), cross_dev, along_dev)
+    across_count, span, substeps, capacity = requests.shape
+
+    if span == 1 and across_count == 4 and capacity % (PIECES * LANES) == 0:
+        moved = advect_twice(fields, requests[:, 0], target, first_fraction, second_fraction)
+    else:
+        asked = to_holders(requests.reshape(across_count, span, substeps * capacity))
+
+        def advect(table, asked, target, fraction):
+            weight = jnp.pad(
+                jnp.tile(fraction.reshape(layers, cells), (components, 1)),
+                ((0, width - row_count), (0, 0)),
+            ).T
+            picked = gather_rows(table, asked.reshape(-1))
+            returned = to_askers(picked.reshape(asked.shape + (width,)))
+            return blend_rows(returned.reshape(-1, width), target, weight, layers)
+
+        table = fields.transpose(1, 0, 2, 3).reshape(row_count, cells)
+        table = jnp.pad(table, ((0, width - row_count), (0, 0))).T
+        middle = advect(table, asked[:, :, :capacity], target[0], first_fraction)
+        moved = advect(middle, asked[:, :, capacity:], target[1], second_fraction)
+        moved = moved.T[:row_count].reshape(components, layers, cross_dev, along_dev)
+        moved = moved.transpose(1, 0, 2, 3)
     padded = padded_2(moved, (("across", 2), ("along", 3)), 1)
     beside_all = neighbour_sum(padded)
     row_total = cross_dev * lax.axis_size("across")

time: 258 us -> 207 us (0.80)
  waiting for transfers between devices: 94.2 us -> 8.34 us
  Pallas kernels: 48.9 us -> 121 us
  local copies, waits for them, and re-layouts: 42.1 us -> 14.7 us
  between operations: 15.6 us -> 28.8 us
  starting transfers between devices: 23.9 us -> 12.4 us
  other arithmetic: 29.5 us -> 21.2 us
    all_to_all x3 -> x0, waiting for transfers between devices: 88.9 us -> none  [the longest x2 88.9 us: to_askers(): lax.all_to_all(picked, 'across', split_axis=0, concat_axis=0, tiled=True)]
    pallas_call x4 -> x1, Pallas kernels: 48.9 us -> 121 us  [advect_twice(): pl.pallas_call(functools.partial(exchange_kernel, layers, components, cro...]
    all_to_all x3 -> x0, starting transfers between devices: 14.9 us -> none  [the longest x2 10 us: to_askers(): lax.all_to_all(picked, 'across', split_axis=0, concat_axis=0, tiled=True)]
    sort x2 -> x0, other arithmetic: 11.6 us -> none  [plan(): ordered = jnp.pad(lax.sort(key) % cells, (0, capacity))]
    transpose x5 -> x0, local copies, waits for them, and re-layouts: 7.89 us -> none  [the longest x2 4.55 us: advect(): weight = jnp.pad(jnp.tile(fraction.reshape(layers, cells), (components, 1...]
    unnamed x51 -> x40, local copies, waits for them, and re-layouts: 10.5 us -> 3.14 us
    ppermute x2, starting transfers between devices: 3.21 us -> 9.22 us  [padded_2(): before = lax.ppermute(last, axis, up)]
    another operation x14 -> x3, local copies, waits for them, and re-layouts: 6.46 us -> 0.74 us  [the longest x1 0.63 us: advect_twice(): grid = requests.reshape(partners, substeps * capacity // LANES, LANES)]
  transfers between devices with their start and end apart: 7 -> 4, of which waited for: 4 -> 3; matrix products, arithmetic and copies ran while one was open for 12% -> 2% of each run, Pallas kernels for 0% -> 0%
where the time goes in v2:
time: 207 us; the launch traced here: 206 us
  Pallas kernels  121 us (58%)
  between operations  28.8 us (14%)
  other arithmetic  21.2 us (10%)
  local copies, waits for them, and re-layouts  14.7 us (7%)
  starting transfers between devices  12.4 us (6%)
  waiting for transfers between devices  8.34 us (4%)
    pallas_call x1, Pallas kernels, advect_twice(): pl.pallas_call(functools.partial(exchange_kernel, layers, components, cro...  121 us
    ppermute x2, starting transfers between devices, padded_2(): before = lax.ppermute(last, axis, up)  9.22 us
    add x1, other arithmetic, body(): mixed = moved + lateral_mix * (beside_all - present * moved)  7.85 us
    slice x2, local copies, waits for them, and re-layouts, padded_2(): last = lax.slice_in_dim(value, length - width, length, axis=dim)  4.7 us
    ppermute x2, waiting for transfers between devices, padded_2(): before = lax.ppermute(last, axis, up)  4.22 us
  transfers between devices with their start and end apart: 4, of which 3 were waited for; matrix products, arithmetic and copies ran while one was open for 2% of the time, Pallas kernels for 0%

profile of v2, /device:TPU:4, one launch (start us, length us, event | category | flops | bytes accessed | tf_op | source)
XLA Modules:
  0.0 206.3 jit_solution(4635583612188127434)
XLA Ops:
  6.5 0.0 copy-start.1
  6.5 0.0 sort.9.cloned.1.call-start
  6.5 0.8 copy.24
  7.4 0.7 copy.25
  8.1 1.0 fusion.50
  9.1 0.0 sort.9.cloned.1.call-update
  9.2 0.1 eq.35
  9.3 0.1 eq.33
  9.4 0.3 convert_reduce_fusion
  9.7 0.2 reduce_window_sum.22
  9.9 0.2 fusion.6
  10.1 0.8 convert_reduce_fusion.1
  10.9 0.2 reduce_window_sum.23
  11.1 0.7 fusion.101
  11.7 0.0 copy-done.1
  11.7 0.1 slice_bitcast_fusion.1
  11.8 0.3 pad_maximum_fusion.8
  12.1 1.5 pad_add_fusion
  13.6 0.5 convert_add_fusion
  29.0 0.0 sort.9.cloned.1.call-done
  29.1 0.8 and_select_fusion
  29.9 0.2 constant_dynamic-slice_fusion
  30.1 0.1 stack.19
  30.1 0.6 reshape_squeeze_reshape.3.requests_ref
  30.8 0.0 copy-start.4
  30.8 120.7 %advect_twice.1 = f32[960,512]{1,0:T(8,128)} custom-call(s32[2,4096]{1,0:T(2,128)} %get-tuple-element.30.target_ref, s32[4,18,128]{2,1,0:T(8,128)} %reshape_squeeze_reshape.3.requests_ref, f32[960,512]{1,0:T(8,128)} %bitcast.50, f32[320,512]{1,0:T(8,128)} %bitcast.51, f32[320,512]{1,0:T(8,128)} %bitcast.52), custom_call_target="tpu_custom_call" | custom-call | tf_op jit(solution)/shard_map/advect_twice/pallas_call | solution.py:433
  151.5 2.6 %fusion.100 = (f32[40,3,1,512]{3,2,1,0:T(1,128)S(1)}, f32[40,3,1,512]{3,2,1,0:T(1,128)S(1)}) fusion(f32[40,3,8,512]{3,2,1,0:T(8,128)} %bitcast.47), kind=kLoop, calls=%fused_computation.324 | loop fusion | bytes 983040 | tf_op jit(solution)/shard_map/slice | solution.py:22
  154.1 6.6 %collective-permute-start = (f32[40,3,1,512]{3,2,1,0:T(1,128)S(1)}, f32[40,3,1,512]{3,2,1,0:T(1,128)S(1)}, u32[]{:S(2)}, u32[]{:S(2)}) collective-permute-start(f32[40,3,1,512]{3,2,1,0:T(1,128)S(1)} %get-tuple-element.134), channel_id=1, source_target_pairs={{0,1},{1,2},{2,3},{4,5},{5,6},{6,7},{8,9},{9,10},{10,11},{12,13},{... | collective-permute-start | bytes 737288 | tf_op jit(solution)/shard_map/ppermute | solution.py:24
  160.8 1.3 collective-permute-start.1
  162.1 0.5 fusion.59
  162.6 0.1 pad.15.clone
  162.7 0.0 copy-start.6
  162.7 0.0 copy-done.4
  162.7 1.7 slice_subtract_fusion.34
  164.3 1.9 collective-permute-done
  166.2 0.0 copy-done.6
  166.2 4.1 %collective-permute-done.1 = f32[40,3,1,512]{3,2,1,0:T(1,128)S(1)} collective-permute-done((f32[40,3,1,512]{3,2,1,0:T(1,128)S(1)}, f32[40,3,1,512]{3,2,1,0:T(1,128)S(1)}, u32[]{:S(2)}, u32[]{:S(2)}) %collective-permute-start.1) | collective-permute-done | bytes 245792 | tf_op jit(solution)/shard_map/ppermute | solution.py:25
  170.3 2.8 %pad_maximum_fusion.11 = (f32[40,3,10,1]{3,2,1,0:T(8,128)}, f32[40,3,10,1]{3,2,1,0:T(8,128)S(1)}) fusion(f32[40,3,1,512]{3,2,1,0:T(1,128)S(1)} %collective-permute-done.1, f32[40,3,8,512]{3,2,1,0:T(8,128)} %bitcast.48, f32[40,3,1,512]{3,2,1,0:T(1,128)S(1)} %collective-permute-done), kind=kLoop, calls=%fused_computation.20 | loop fusion | flops 4800 | bytes 2467200 | tf_op jit(solution)/shard_map/slice | solution.py:22
  173.1 2.1 %copy.20 = f32[40,3,10,1]{0,3,2,1:T(1,128)} copy(f32[40,3,10,1]{3,2,1,0:T(8,128)} %get-tuple-element.132) | data formatting | bytes 9600 | tf_op jit(solution)/shard_map/slice | solution.py:22
  175.1 0.9 copy.22
  176.0 1.9 collective-permute-start.3
  178.0 2.6 %collective-permute-start.2 = (f32[40,3,10,1]{0,3,2,1:T(1,128)}, f32[40,3,10,1]{0,3,2,1:T(1,128)}, u32[]{:S(2)}, u32[]{:S(2)}) collective-permute-start(f32[40,3,10,1]{0,3,2,1:T(1,128)} %copy.20), channel_id=1, source_target_pairs={{0,4},{4,8},{8,12},{12,16},{16,20},{20,24},{24,28},{1,5},{5,9},{9,... | collective-permute-start | bytes 14408 | tf_op jit(solution)/shard_map/ppermute | solution.py:24
  180.6 1.3 broadcast_add_fusion
  181.9 2.4 %collective-permute-done.2 = f32[40,3,10,1]{0,3,2,1:T(1,128)} collective-permute-done((f32[40,3,10,1]{0,3,2,1:T(1,128)}, f32[40,3,10,1]{0,3,2,1:T(1,128)}, u32[]{:S(2)}, u32[]{:S(2)}) %collective-permute-start.2) | collective-permute-done | bytes 4832 | tf_op jit(solution)/shard_map/ppermute | solution.py:24
  184.2 1.2 copy.21
  185.5 0.0 collective-permute-done.3
  185.5 2.1 %copy.23 = f32[40,3,10,1]{3,2,1,0:T(8,128)} copy(f32[40,3,10,1]{0,3,2,1:T(1,128)} %collective-permute-done.3) | data formatting | bytes 9600 | tf_op jit(solution)/shard_map/ppermute | solution.py:25
  187.6 0.0 copy-start.5
  187.6 0.0 copy-start
  187.6 0.0 copy-start.7
  187.6 7.8 %fusion.3 = f32[40,3,8,512]{3,2,1,0:T(8,128)S(1)} fusion(f32[40,3,8,512]{3,2,1,0:T(8,128)} %bitcast.49, f32[40,3,10,1]{3,2,1,0:T(8,128)} %copy.23, f32[40,3,1,512]{3,2,1,0:T(1,128)S(1)} %collective-permute-done.1, f32[40,3,1,512]{3,2,1,0:T(1,128)S(1)} %collective-permute-done, f32[40,3,10,1]{3,2,1,0:T(8,128)S(1)} %copy.21, f32[8,512]{1,0:T(8,128)} %broadcast_add_fusion, ...), kind=kLoop, calls=%fused_computation.4 | loop fusion | flops 7372800 | bytes 4466048 | tf_op jit(solution)/shard_map/add | solution.py:526
  195.4 0.0 copy-done.5
  195.5 0.0 copy-done
  195.5 0.0 copy-done.7
  195.5 0.1 fusion.43
  195.6 0.0 copy-start.2
  195.6 0.0 copy-start.3
  195.6 0.7 fusion.10
  196.3 0.1 copy-done.2
  196.4 0.0 copy-done.3
  196.4 0.5 constant_dynamic-update-slice_fusion.39
  197.6 0.0 copy-start.8
  197.6 1.3 copy-done.8
  198.8 0.6 constant_dynamic-update-slice_fusion
  (46 shorter events, 0.5 us)
Async XLA Ops:
  6.5 5.2 %copy-start.1 = (f32[2,39,8,512]{3,2,1,0:T(8,128)S(1)}, f32[2,39,8,512]{3,2,1,0:T(8,128)}, u32[]{:S(2)}) copy-start(f32[2,39,8,512]{3,2,1,0:T(8,128)} %param.19) | copy-start | bytes 3833860
  6.5 22.5 %sort.9.cloned.1.call-start = ((), (), s32[]{:S(2)}) async-start(), calls=%async_computation | async-start | bytes 98336 | tf_op jit(solution)/shard_map/sort | solution.py:99
  30.8 131.9 %copy-start.4 = (f32[8,512]{1,0:T(8,128)S(1)}, f32[8,512]{1,0:T(8,128)}, u32[]{:S(2)}) copy-start(f32[8,512]{1,0:T(8,128)} %param.20) | copy-start | bytes 49156
  154.1 12.0 %collective-permute-start = (f32[40,3,1,512]{3,2,1,0:T(1,128)S(1)}, f32[40,3,1,512]{3,2,1,0:T(1,128)S(1)}, u32[]{:S(2)}, u32[]{:S(2)}) collective-permute-start(f32[40,3,1,512]{3,2,1,0:T(1,128)S(1)} %get-tuple-element.134), channel_id=1, source_target_pairs={{0,1},{1,2},{2,3},{4,5},{5,6},{6,7},{8,9},{9,10},{10,11},{12,13},{... | collective-permute-start | bytes 737288 | tf_op jit(solution)/shard_map/ppermute | solution.py:24
  160.8 9.5 %collective-permute-start.1 = (f32[40,3,1,512]{3,2,1,0:T(1,128)S(1)}, f32[40,3,1,512]{3,2,1,0:T(1,128)S(1)}, u32[]{:S(2)}, u32[]{:S(2)}) collective-permute-start(f32[40,3,1,512]{3,2,1,0:T(1,128)S(1)} %get-tuple-element.135), channel_id=1, source_target_pairs={{1,0},{2,1},{3,2},{5,4},{6,5},{7,6},{9,8},{10,9},{11,10},{13,12},{... | collective-permute-start | bytes 737288 | tf_op jit(solution)/shard_map/ppermute | solution.py:25
  162.7 3.5 %copy-start.6 = (f32[3]{0:T(128)}, f32[3]{0:T(128)S(1)}, u32[]{:S(2)}) copy-start(f32[3]{0:T(128)S(1)} %pad.15.clone) | copy-start | bytes 40
  176.0 9.4 %collective-permute-start.3 = (f32[40,3,10,1]{0,3,2,1:T(1,128)}, f32[40,3,10,1]{0,3,2,1:T(1,128)}, u32[]{:S(2)}, u32[]{:S(2)}) collective-permute-start(f32[40,3,10,1]{0,3,2,1:T(1,128)} %copy.22), channel_id=1, source_target_pairs={{4,0},{8,4},{12,8},{16,12},{20,16},{24,20},{28,24},{5,1},{9,5},{13... | collective-permute-start | bytes 14408 | tf_op jit(solution)/shard_map/ppermute | solution.py:25
  178.0 6.3 %collective-permute-start.2 = (f32[40,3,10,1]{0,3,2,1:T(1,128)}, f32[40,3,10,1]{0,3,2,1:T(1,128)}, u32[]{:S(2)}, u32[]{:S(2)}) collective-permute-start(f32[40,3,10,1]{0,3,2,1:T(1,128)} %copy.20), channel_id=1, source_target_pairs={{0,4},{4,8},{8,12},{12,16},{16,20},{20,24},{24,28},{1,5},{5,9},{9,... | collective-permute-start | bytes 14408 | tf_op jit(solution)/shard_map/ppermute | solution.py:24
  187.6 7.9 %copy-start.5 = (f32[2,8,512]{2,1,0:T(8,128)S(1)}, f32[2,8,512]{2,1,0:T(8,128)}, u32[]{:S(2)}) copy-start(f32[2,8,512]{2,1,0:T(8,128)} %param.21) | copy-start | bytes 98308
  187.6 7.9 %copy-start = (f32[40,3,8,512]{3,2,1,0:T(8,128)S(1)}, f32[40,3,8,512]{3,2,1,0:T(8,128)}, u32[]{:S(2)}) copy-start(f32[40,3,8,512]{3,2,1,0:T(8,128)} %pad_add_fusion) | copy-start | bytes 5898244
  187.6 7.9 %copy-start.7 = (f32[3]{0:T(128)S(1)}, f32[3]{0:T(128)}, u32[]{:S(2)}) copy-start(f32[3]{0:T(128)} %copy-done.6) | copy-start | bytes 40
  195.6 0.8 copy-start.2
  195.6 0.8 copy-start.3
  197.6 1.3 copy-start.8
Sparse Core Ops, SparseCore 0:
  9.8 11.4 sort.11.cloned.1.call-done
  (1 shorter events, 0.0 us)

commit v3 on v2

--- a/solution.py
+++ b/solution.py
@@ -96,7 +96,7 @@
     offset = owner_along - lax.axis_index("along")
     partner = owner_across * span + offset + reach - 1
     key = (partner * cells + jnp.arange(cells, dtype=jnp.int32)) * cells + local_cell
-    ordered = jnp.pad(lax.sort(key, dimension=1) % cells, ((0, 0), (0, capacity)))
+    ordered = [jnp.pad(lax.sort(key[s]) % cells, (0, capacity)) for s in range(substeps)]
     labels = jnp.arange(partners, dtype=jnp.int32)[:, None]
     member = (partner[:, None, :] == labels).astype(jnp.int32)
     rank, counts = prefix_count(member.reshape(substeps * partners, cells))
@@ -216,11 +216,14 @@
     fields_hbm,
     first_hbm,
     second_hbm,
-    out_hbm,
+    out_ref,
+    west_ref,
+    east_ref,
+    north_ref,
+    south_ref,
     fields_ref,
     first_ref,
     second_ref,
-    out_ref,
     asked_vmem,
     asked,
     table,
@@ -239,6 +242,14 @@
     send_sem,
     recv_sem,
     load_sem,
+    edge_w,
+    edge_e,
+    halo_n,
+    halo_s,
+    halo_w,
+    halo_e,
+    halo_send,
+    halo_recv,
 ):
     tiles = fields_ref.shape[0]
     along_dev = tiles * LANES
@@ -270,7 +281,19 @@
     barrier = pltpu.get_barrier_semaphore()
     for peer in peers:
         pl.semaphore_signal(barrier, inc=1, device_id=(along, peer), device_id_type=MESH)
-    pl.semaphore_wait(barrier, 3)
+    along_count = lax.axis_size("along")
+    has_west, has_east = along > 0, along < along_count - 1
+    has_north, has_south = me > 0, me < lax.axis_size("across") - 1
+
+    @pl.when(has_west)
+    def _():
+        pl.semaphore_signal(barrier, inc=1, device_id=(along - 1, me), device_id_type=MESH)
+
+    @pl.when(has_east)
+    def _():
+        pl.semaphore_signal(barrier, inc=1, device_id=(along + 1, me), device_id_type=MESH)
+
+    pl.semaphore_wait(barrier, 3 + has_west.astype(jnp.int32) + has_east.astype(jnp.int32))
 
     asks = []
     for j, peer in enumerate(peers):
@@ -386,35 +409,111 @@
     exchange(gather_1, 0, sent_1, back_1, weights)
     exchange(gather_2, 1, sent_2, back_2, lambda: None)
 
-    def last(b, carry):
-        start = pl.multiple_of(b * LANES, LANES)
+    def unpack(start):
+        start = pl.multiple_of(start, LANES)
         for u in range(LANES):
             final[pl.ds(start + u, 1), :] = back_2[pl.ds(target_ref[1, start + u], 1), :]
+        rows = pl.ds(start, LANES)
+        final[rows, :] = blend(final[rows, :], second_rows[rows, :], top)
+
+    def unpack_row(first):
+        def step(t, carry):
+            unpack(first + t * LANES)
+            return carry
+
+        lax.fori_loop(0, tiles, step, 0)
+
+    def halo(j, source, place, peer):
+        return pltpu.make_async_remote_copy(
+            src_ref=source,
+            dst_ref=place,
+            send_sem=halo_send.at[j],
+            recv_sem=halo_recv.at[j],
+            device_id=peer,
+            device_id_type=MESH,
+        )
+
+    top_row, last_row = pl.ds(0, along_dev), pl.ds(cells - along_dev, along_dev)
+    north = halo(0, final.at[top_row], halo_s, (along, me - 1))
+    south = halo(1, final.at[last_row], halo_n, (along, me + 1))
+    west = halo(2, edge_w, halo_e, (along - 1, me))
+    east = halo(3, edge_e, halo_w, (along + 1, me))
+
+    unpack_row(0)
+    unpack_row(cells - along_dev)
+    inner = cross_dev - 2
+
+    def outer_columns(i, carry):
+        unpack((i + 1) * along_dev)
+        unpack((i + 2) * along_dev - LANES)
         return carry
 
-    lax.fori_loop(0, cells // LANES, last, 0)
+    lax.fori_loop(0, inner, outer_columns, 0)
+
+    for i in range(cross_dev):
+        edge_w[pl.ds(i, 1), :] = final[pl.ds(i * along_dev, 1), :]
+        edge_e[pl.ds(i, 1), :] = final[pl.ds((i + 1) * along_dev - 1, 1), :]
+
+    for present, copy in [
+        (has_north, north), (has_south, south), (has_west, west), (has_east, east)
+    ]:
+        @pl.when(present)
+        def _(copy=copy):
+            copy.start()
+
+    def inner_columns(i, carry):
+        def step(t, carry):
+            unpack((i + 1) * along_dev + (t + 1) * LANES)
+            return carry
+
+        return lax.fori_loop(0, tiles - 2, step, carry)
+
+    lax.fori_loop(0, inner, inner_columns, 0)
+
+    def spread(value, ref, first, stride, t):
+        for m in range(components):
+            ref[t, pl.ds(m * stride + first, layers, stride=components * stride), :] = value[
+                m * layers : (m + 1) * layers
+            ]
 
     def emit(i, carry):
         for t in range(tiles):
             rows = pl.ds(pl.multiple_of(i * along_dev + t * LANES, LANES), LANES)
-            value = blend(final[rows, :], second_rows[rows, :], top).T
-            for m in range(components):
-                out_ref[
-                    t, pl.ds(m * cross_dev + i, layers, stride=components * cross_dev), :
-                ] = value[m * layers : (m + 1) * layers]
+            spread(final[rows, :].T, out_ref, i, cross_dev, t)
         return carry
 
     lax.fori_loop(0, cross_dev, emit, 0)
-    stores = [
-        pltpu.make_async_copy(
-            out_ref.at[t], out_hbm.at[:, pl.ds(t * LANES, LANES)], load_sem.at[3, t]
-        )
-        for t in range(tiles)
-    ]
-    for copy in stores:
-        copy.start()
-    for copy in stores:
-        copy.wait()
+
+    for present, copy, place in [
+        (has_south, north, halo_s),
+        (has_north, south, halo_n),
+        (has_east, west, halo_e),
+        (has_west, east, halo_w),
+    ]:
+        @pl.when(present)
+        def _(copy=copy):
+            copy.wait_recv()
+
+        @pl.when(jnp.logical_not(present))
+        def _(place=place):
+            place[...] = jnp.zeros_like(place)
+
+    for t in range(tiles):
+        rows = pl.ds(t * LANES, LANES)
+        spread(halo_n[rows, :].T, north_ref, 0, 1, t)
+        spread(halo_s[rows, :].T, south_ref, 0, 1, t)
+    for i in range(cross_dev):
+        for source, place in [(halo_w, west_ref), (halo_e, east_ref)]:
+            row = jnp.broadcast_to(source[pl.ds(i, 1), :], (LANES, width))
+            spread(row.T, place, i, cross_dev, 0)
+
+    for present, copy in [
+        (has_north, north), (has_south, south), (has_west, west), (has_east, east)
+    ]:
+        @pl.when(present)
+        def _(copy=copy):
+            copy.wait_send()
+
     for copy in asks:
         copy.wait_send()
 
@@ -430,16 +529,23 @@
     tiles = along_dev // LANES
     grid = requests.reshape(partners, substeps * capacity // LANES, LANES)
     rows = lambda count: pltpu.VMEM((count, width), jnp.float32)
-    moved = pl.pallas_call(
+    shape = lambda *dims: jax.ShapeDtypeStruct(dims, jnp.float32)
+    edge = layers * components
+    return pl.pallas_call(
         functools.partial(exchange_kernel, layers, components, cross_dev, capacity),
-        out_shape=jax.ShapeDtypeStruct((layers * components * cross_dev, along_dev), jnp.float32),
+        out_shape=[
+            shape(tiles, edge * cross_dev, LANES),
+            shape(1, edge * cross_dev, LANES),
+            shape(1, edge * cross_dev, LANES),
+            shape(tiles, edge, LANES),
+            shape(tiles, edge, LANES),
+        ],
         in_specs=[smem, vmem, hbm, hbm, hbm],
-        out_specs=hbm,
+        out_specs=[vmem] * 5,
         scratch_shapes=[
             pltpu.VMEM((tiles, layers * components * cross_dev, LANES), jnp.float32),
             pltpu.VMEM((tiles, layers * cross_dev, LANES), jnp.float32),
             pltpu.VMEM((tiles, layers * cross_dev, LANES), jnp.float32),
-            pltpu.VMEM((tiles, layers * components * cross_dev, LANES), jnp.float32),
             pltpu.VMEM(grid.shape, jnp.int32),
             pltpu.SMEM(grid.shape, jnp.int32),
             rows(cells),
@@ -457,7 +563,15 @@
             pltpu.SemaphoreType.DMA((4,)),
             pltpu.SemaphoreType.DMA((2, 3, PIECES)),
             pltpu.SemaphoreType.DMA((2, 3, PIECES)),
-            pltpu.SemaphoreType.DMA((4, tiles)),
+            pltpu.SemaphoreType.DMA((3, tiles)),
+            rows(cross_dev),
+            rows(cross_dev),
+            rows(along_dev),
+            rows(along_dev),
+            rows(cross_dev),
+            rows(cross_dev),
+            pltpu.SemaphoreType.DMA((4,)),
+            pltpu.SemaphoreType.DMA((4,)),
         ],
         compiler_params=pltpu.CompilerParams(collective_id=0, has_side_effects=True),
         name="advect_twice",
@@ -468,7 +582,119 @@
         first_fraction.reshape(layers * cross_dev, along_dev),
         second_fraction.reshape(layers * cross_dev, along_dev),
     )
-    return moved.reshape(fields.shape)
+
+
+def solve_kernel(
+    layers,
+    components,
+    moved_ref,
+    west_ref,
+    east_ref,
+    north_ref,
+    south_ref,
+    present_ref,
+    lateral_ref,
+    mix_ref,
+    drag_ref,
+    stress_ref,
+    out_ref,
+    factors,
+):
+    cross_dev = out_ref.shape[2]
+    tiles = moved_ref.shape[0]
+    lane = lax.broadcasted_iota(jnp.int32, (cross_dev, LANES), 1)
+    row = lax.broadcasted_iota(jnp.int32, (cross_dev, LANES), 0)
+    at = [pl.ds(t * LANES, LANES) for t in range(tiles)]
+    lateral = [lateral_ref[:, at[t]] for t in range(tiles)]
+    present = [present_ref[:, at[t]] for t in range(tiles)]
+
+    def mixed(k, m):
+        level = k * components + m
+        rows = pl.ds(pl.multiple_of(level * cross_dev, cross_dev), cross_dev)
+        here = [moved_ref[t, rows, :] for t in range(tiles)]
+        right = [pltpu.roll(x, 1, 1) for x in [west_ref[0, rows, :]] + here]
+        left = [pltpu.roll(x, LANES - 1, 1) for x in here + [east_ref[0, rows, :]]]
+        result = []
+        for t in range(tiles):
+            x = here[t]
+            before = jnp.where(lane == 0, right[t], right[t + 1])
+            after = jnp.where(lane == LANES - 1, left[t + 1], left[t])
+            above = jnp.where(
+                row == 0, north_ref[t, pl.ds(level, 1), :], pltpu.roll(x, 1, 0)
+            )
+            below = jnp.where(
+                row == cross_dev - 1,
+                south_ref[t, pl.ds(level, 1), :],
+                pltpu.roll(x, cross_dev - 1, 0),
+            )
+            total = above + below + before + after
+            result.append(x + lateral[t] * (total - present[t] * x))
+        return result
+
+    def forward(k, carry, first=False, final=False):
+        factor, partial = carry or (None, None)
+        source = [mixed(k, m) for m in range(components)]
+        new_factor, new_partial = [], [None] * components
+        for g in range(2):
+            members = (0, 1) if g == 0 else (2,)
+            row_factor = []
+            for t in range(tiles):
+                above = 0.0 if final else mix_ref[g, k, :, at[t]]
+                below = 0.0 if first else mix_ref[g, k - 1, :, at[t]]
+                diagonal = 1.0 + below + above
+                if first:
+                    if g == 0:
+                        diagonal = diagonal + drag_ref[:, at[t]]
+                else:
+                    diagonal = diagonal - below * factor[g][t]
+                inverse = 1.0 / diagonal
+                for m in members:
+                    value = source[m][t]
+                    if final and g == 0:
+                        value = value + stress_ref[m, :, at[t]]
+                    if not first:
+                        value = value + below * partial[m][t]
+                    value = value * inverse
+                    new_partial[m] = (new_partial[m] or []) + [value]
+                    out_ref[k, m, :, at[t]] = value
+                if not final:
+                    ratio = above * inverse
+                    factors[g, k, :, at[t]] = ratio
+                    row_factor.append(ratio)
+            new_factor.append(row_factor)
+        return new_factor, new_partial
+
+    carry = forward(0, None, first=True)
+    carry = lax.fori_loop(1, layers - 1, forward, carry)
+    _, value = forward(layers - 1, carry, final=True)
+
+    def backward(step, value):
+        k = layers - 2 - step
+        result = []
+        for m in range(components):
+            g = 0 if m < 2 else 1
+            level = []
+            for t in range(tiles):
+                x = out_ref[k, m, :, at[t]] + factors[g, k, :, at[t]] * value[m][t]
+                out_ref[k, m, :, at[t]] = x
+                level.append(x)
+            result.append(level)
+        return result
+
+    lax.fori_loop(0, layers - 1, backward, value)
+
+
+def mix_and_solve(pieces, present, lateral_mix, vertical_mix, bottom_drag, surface_stress, shape):
+    layers, components, cross_dev, along_dev = shape
+    vmem = pl.BlockSpec(memory_space=pltpu.VMEM)
+    return pl.pallas_call(
+        functools.partial(solve_kernel, layers, components),
+        out_shape=jax.ShapeDtypeStruct(shape, jnp.float32),
+        in_specs=[vmem] * 10,
+        out_specs=vmem,
+        scratch_shapes=[pltpu.VMEM((2, layers - 1, cross_dev, along_dev), jnp.float32)],
+        name="mix_and_solve",
+    )(*pieces, present, lateral_mix, vertical_mix, bottom_drag, surface_stress)
 
 
 def body(
@@ -490,28 +716,6 @@
     requests, target = plan(jnp.stack([first_feet, second_feet]), cross_dev, along_dev)
     across_count, span, substeps, capacity = requests.shape
 
-    if span == 1 and across_count == 4 and capacity % (PIECES * LANES) == 0:
-        moved = advect_twice(fields, requests[:, 0], target, first_fraction, second_fraction)
-    else:
-        asked = to_holders(requests.reshape(across_count, span, substeps * capacity))
-
-        def advect(table, asked, target, fraction):
-            weight = jnp.pad(
-                jnp.tile(fraction.reshape(layers, cells), (components, 1)),
-                ((0, width - row_count), (0, 0)),
-            ).T
-            picked = gather_rows(table, asked.reshape(-1))
-            returned = to_askers(picked.reshape(asked.shape + (width,)))
-            return blend_rows(returned.reshape(-1, width), target, weight, layers)
-
-        table = fields.transpose(1, 0, 2, 3).reshape(row_count, cells)
-        table = jnp.pad(table, ((0, width - row_count), (0, 0))).T
-        middle = advect(table, asked[:, :, :capacity], target[0], first_fraction)
-        moved = advect(middle, asked[:, :, capacity:], target[1], second_fraction)
-        moved = moved.T[:row_count].reshape(components, layers, cross_dev, along_dev)
-        moved = moved.transpose(1, 0, 2, 3)
-    padded = padded_2(moved, (("across", 2), ("along", 3)), 1)
-    beside_all = neighbour_sum(padded)
     row_total = cross_dev * lax.axis_size("across")
     column_total = along_dev * lax.axis_size("along")
     row_index = lax.axis_index("across") * cross_dev + jnp.arange(cross_dev, dtype=jnp.int32)
@@ -523,6 +727,37 @@
         column_index < column_total - 1
     ).astype(jnp.float32)
     present = row_present[:, None] + column_present[None, :]
+    if span == 1 and across_count == 4 and capacity % (PIECES * LANES) == 0:
+        pieces = advect_twice(fields, requests[:, 0], target, first_fraction, second_fraction)
+        return mix_and_solve(
+            pieces,
+            present,
+            lateral_mix,
+            vertical_mix,
+            bottom_drag,
+            surface_stress,
+            fields.shape,
+        )
+    else:
+        asked = to_holders(requests.reshape(across_count, span, substeps * capacity))
+
+        def advect(table, asked, target, fraction):
+            weight = jnp.pad(
+                jnp.tile(fraction.reshape(layers, cells), (components, 1)),
+                ((0, width - row_count), (0, 0)),
+            ).T
+            picked = gather_rows(table, asked.reshape(-1))
+            returned = to_askers(picked.reshape(asked.shape + (width,)))
+            return blend_rows(returned.reshape(-1, width), target, weight, layers)
+
+        table = fields.transpose(1, 0, 2, 3).reshape(row_count, cells)
+        table = jnp.pad(table, ((0, width - row_count), (0, 0))).T
+        middle = advect(table, asked[:, :, :capacity], target[0], first_fraction)
+        moved = advect(middle, asked[:, :, capacity:], target[1], second_fraction)
+        moved = moved.T[:row_count].reshape(components, layers, cross_dev, along_dev)
+        moved = moved.transpose(1, 0, 2, 3)
+    padded = padded_2(moved, (("across", 2), ("along", 3)), 1)
+    beside_all = neighbour_sum(padded)
     mixed = moved + lateral_mix * (beside_all - present * moved)
     return solve_columns(mixed, vertical_mix, bottom_drag, surface_stress)
 

time: 207 us -> 170 us (0.82)
  Pallas kernels: 121 us -> 135 us
  between operations: 28.8 us -> 15 us
  starting transfers between devices: 12.4 us -> 0 us
  local copies, waits for them, and re-layouts: 14.7 us -> 3.38 us
  waiting for transfers between devices: 8.34 us -> 0 us
  other arithmetic: 21.2 us -> 14.1 us
    ppermute x4 -> x0, starting transfers between devices: 12.4 us -> none  [the longest x2 9.22 us: padded_2(): before = lax.ppermute(last, axis, up)]
    sort x0 -> x2, other arithmetic: none -> 11.6 us  [plan(): lax.sort(key[s]) % cells]
    add x2 -> x0, other arithmetic: 9.38 us -> none  [the longest x1 7.85 us: body(): mixed = moved + lateral_mix * (beside_all - present * moved)]
    pallas_call x0 -> x1, Pallas kernels: none -> 8.37 us  [mix_and_solve(): pl.pallas_call(functools.partial(solve_kernel, layers, components), out_s...]
    ppermute x4 -> x0, waiting for transfers between devices: 8.34 us -> none  [the longest x2 4.22 us: padded_2(): before = lax.ppermute(last, axis, up)]
    pallas_call x1, Pallas kernels: 121 us -> 127 us  [advect_twice(): pl.pallas_call(functools.partial(exchange_kernel, layers, components, cro...]
    slice x4 -> x1, local copies, waits for them, and re-layouts: 5.64 us -> 0.03 us  [plan(): key[s]]
    ppermute x2 -> x0, local copies, waits for them, and re-layouts: 3.32 us -> none  [the longest x1 2.11 us: padded_2(): after = lax.ppermute(first, axis, down)]
  transfers between devices with their start and end apart: 4 -> 0, of which waited for: 3 -> 0; matrix products, arithmetic and copies ran while one was open for 2% -> 0% of each run, Pallas kernels for 0% -> 0%
where the time goes in v3:
time: 170 us; the launch traced here: 168 us
  Pallas kernels  135 us (79%)
  between operations  15 us (9%)
  other arithmetic  14.1 us (8%)
  local copies, waits for them, and re-layouts  3.38 us (2%)
    pallas_call x1, Pallas kernels, advect_twice(): pl.pallas_call(functools.partial(exchange_kernel, layers, components, cro...  127 us
    sort x2, other arithmetic, plan(): lax.sort(key[s]) % cells  11.6 us
    pallas_call x1, Pallas kernels, mix_and_solve(): pl.pallas_call(functools.partial(solve_kernel, layers, components), out_s...  8.37 us

profile of v3, /device:TPU:4, one launch (start us, length us, event | category | flops | bytes accessed | tf_op | source)
XLA Modules:
  0.0 168.0 jit_solution(8856132323835943000)
XLA Ops:
  0.0 0.1 eq.37
  0.1 0.7 broadcast_add_fusion.present_ref
  0.8 0.7 copy.10
  1.5 0.7 copy.11
  2.3 0.4 fusion.5
  2.7 5.8 %sort.28 = (s32[4096]{0:T(1024)S(1)}, s32[4096]{0:T(1024)}) sort(s32[4096]{0:T(1024)S(1)} %bitcast.28, s32[4096]{0:T(1024)S(1)} %iota.48), dimensions={0}, to_apply=%region_3.4 | sort | flops 49152 | bytes 65536 | tf_op jit(solution)/shard_map/sort | solution.py:99
  8.5 5.8 %sort.29 = (s32[4096]{0:T(1024)S(1)}, s32[4096]{0:T(1024)}) sort(s32[4096]{0:T(1024)S(1)} %bitcast.25, s32[4096]{0:T(1024)S(1)} %iota.49), dimensions={0}, to_apply=%region_6.7 | sort | flops 49152 | bytes 65536 | tf_op jit(solution)/shard_map/sort | solution.py:99
  14.3 0.1 eq.35
  14.4 0.3 convert_reduce_fusion
  14.7 0.2 reduce_window_sum.22
  14.9 0.2 fusion
  15.1 0.8 convert_reduce_fusion.1
  15.9 0.2 reduce_window_sum.23
  16.1 0.7 fusion.19
  31.6 0.1 pad_dynamic-slice_fusion
  31.8 0.1 pad_dynamic-slice_fusion.4
  31.9 0.1 stack.47
  32.0 0.6 reshape_squeeze_reshape.3.requests_ref
  32.6 127.0 %advect_twice.1 = (f32[4,960,128]{2,1,0:T(8,128)}, f32[1,960,128]{2,1,0:T(8,128)}, f32[1,960,128]{2,1,0:T(8,128)}, f32[4,120,128]{2,1,0:T(8,128)}, f32[4,120,128]{2,1,0:T(8,128)}) custom-call(s32[2,4096]{1,0:T(2,128)} %get-tuple-element.22.target_ref, s32[4,18,128]{2,1,0:T(8,128)} %reshape_squeeze_reshape.3.requests_ref, f32[960,512]{1,0:T(8,128)} %bitcast.22, ...), custom_call_target="tpu_custom_call" | custom-call | tf_op jit(solution)/shard_map/advect_twice/pallas_call | solution.py:534
  159.6 8.4 %mix_and_solve.1 = f32[40,3,8,512]{3,2,1,0:T(8,128)} custom-call(f32[4,960,128]{2,1,0:T(8,128)} %get-tuple-element.16.moved_ref, f32[1,960,128]{2,1,0:T(8,128)} %get-tuple-element.17.west_ref, f32[1,960,128]{2,1,0:T(8,128)} %get-tuple-element.18.east_ref, f32[4,120,128]{2,1,0:T(8,128)} %get-tuple-element.19.north_ref, ...), custom_call_target="tpu_custom_call" | custom-call | tf_op jit(solution)/shard_map/mix_and_solve/pallas_call | solution.py:690
  (21 shorter events, 0.2 us)

commit v4 on v3

--- a/solution.py
+++ b/solution.py
@@ -81,6 +81,41 @@
     return (inside + ahead[:, :, None]).reshape(partners, cells), totals.sum(axis=1)
 
 
+LANES = 128
+
+
+def cut_kernel(capacity, starts_ref, ordered_ref, out_ref):
+    partners, substeps = out_ref.shape[:2]
+    blocks = capacity // LANES
+    lane = lax.broadcasted_iota(jnp.int32, (blocks, LANES), 1)
+    for p in range(partners):
+        for s in range(substeps):
+            start = starts_ref[s, p]
+            first = start // LANES
+            shift = start - first * LANES
+            rows = ordered_ref[s, pl.ds(first, blocks + 7), :]
+            turned = pltpu.roll(rows, lax.rem(LANES - shift, LANES), 1)
+            out_ref[p, s] = jnp.where(
+                lane < LANES - shift, turned[:blocks], turned[1 : blocks + 1]
+            )
+
+
+def cut_requests(ordered, starts, capacity):
+    substeps, length = ordered.shape
+    rows = (length + 8 * LANES - 1) // LANES + 7
+    ordered = jnp.pad(ordered, ((0, 0), (0, rows * LANES - length)))
+    vmem = pl.BlockSpec(memory_space=pltpu.VMEM)
+    return pl.pallas_call(
+        functools.partial(cut_kernel, capacity),
+        out_shape=jax.ShapeDtypeStruct(
+            (starts.shape[1], substeps, capacity // LANES, LANES), jnp.int32
+        ),
+        in_specs=[pl.BlockSpec(memory_space=pltpu.SMEM), vmem],
+        out_specs=vmem,
+        name="cut_requests",
+    )(starts, ordered.reshape(substeps, rows, LANES))
+
+
 def plan(feet, cross_dev, along_dev):
     along_count = lax.axis_size("along")
     across_count = lax.axis_size("across")
@@ -104,6 +139,9 @@
     target = jnp.sum(member * (rank + capacity * labels), axis=1)
     counts = counts.reshape(substeps, partners)
     starts = jnp.cumsum(counts, axis=1) - counts
+    if capacity % LANES == 0:
+        requests = cut_requests(jnp.stack(ordered), starts, capacity)
+        return requests.reshape(across_count, span, substeps, capacity), target
     requests = [
         lax.dynamic_slice(ordered[s], (starts[s, p],), (capacity,))
         for p in range(partners)
@@ -196,7 +234,6 @@
     return lax.all_to_all(picked, "across", split_axis=0, concat_axis=0, tiled=True)
 
 
-LANES = 128
 PIECES = 3
 MESH = pl.DeviceIdType.MESH
 
@@ -231,6 +268,8 @@
     second_rows,
     sent_1,
     sent_2,
+    raw_1,
+    raw_2,
     back_1,
     back_2,
     stage,
@@ -344,61 +383,70 @@
     for copy in locals_ + [own]:
         copy.wait()
 
-    def gather_1(peer, c, dst, base):
-        def step(b, carry):
-            row = c * (piece // LANES) + b
-            start = pl.multiple_of(base + b * LANES, LANES)
-            for u in range(LANES):
-                dst[pl.ds(start + u, 1), :] = table[pl.ds(asked[peer, row, u], 1), :]
-            return carry
-
-        lax.fori_loop(0, piece // LANES, step, 0)
-
-    def gather_2(peer, c, dst, base):
-        def step(b, carry):
-            row = blocks + c * (piece // LANES) + b
-            start = pl.multiple_of(base + b * LANES, LANES)
-            for u in range(LANES):
-                cell = asked[peer, row, u]
-                stage[pl.ds(u, 1), :] = back_1[pl.ds(target_ref[0, cell], 1), :]
-                stage_weight[pl.ds(u, 1), :] = first_rows[pl.ds(cell, 1), :]
-            dst[pl.ds(start, LANES), :] = blend(stage[...], stage_weight[...], top)
-            return carry
-
-        lax.fori_loop(0, piece // LANES, step, 0)
-
-    def exchange(gather, phase, sent, back, beside):
-        copies = []
-        for c in range(PIECES):
-            for j, peer in enumerate(peers[:2]):
-                copies.append((j, peer, c))
-        for c in range(PIECES):
-            copies.append((2, peers[2], c))
+    steps = piece // LANES
+
+    def gather_1(peer, row):
+        for u in range(LANES):
+            stage[pl.ds(u, 1), :] = table[pl.ds(asked[peer, row, u], 1), :]
+        return stage[...]
+
+    def gather_2(peer, row):
+        for u in range(LANES):
+            cell = asked[peer, blocks + row, u]
+            stage[pl.ds(u, 1), :] = back_1[pl.ds(target_ref[0, cell], 1), :]
+            stage_weight[pl.ds(u, 1), :] = first_rows[pl.ds(cell, 1), :]
+        return blend(stage[...], stage_weight[...], top)
+
+    def exchange(gather, phase, sent, raw, back, beside):
+        copies = [(j, c) for c in range(PIECES) for j in range(2)]
+        copies += [(2, c) for c in range(PIECES)]
         started = []
         waiting = None
-        for j, peer, c in copies:
-            base = j * capacity + c * piece
-            gather(peer, c, sent, base)
+        for j, c in copies:
+            slot = j * PIECES + c
+
+            def step(b, carry, j=j, c=c, slot=slot):
+                columns = gather(peers[j], c * steps + b).T[: layers * components]
+                sent[slot, :, pl.ds(pl.multiple_of(b * LANES, LANES), LANES)] = columns
+                return carry
+
+            lax.fori_loop(0, steps, step, 0)
             copy = pltpu.make_async_remote_copy(
-                src_ref=sent.at[pl.ds(base, piece)],
-                dst_ref=back.at[pl.ds(pl.multiple_of(me * capacity + c * piece, LANES), piece)],
+                src_ref=sent.at[slot],
+                dst_ref=raw.at[slot],
                 send_sem=send_sem.at[phase, j, c],
                 recv_sem=recv_sem.at[phase, j, c],
-                device_id=(along, peer),
+                device_id=(along, peers[j]),
                 device_id_type=MESH,
             )
             if waiting is not None:
                 waiting.start()
             waiting = copy
             started.append(copy)
-        for c in range(PIECES):
-            gather(me, c, back, me * capacity + c * piece)
-            if waiting is not None:
-                waiting.start()
-                waiting = None
+
+        def keep(b, carry):
+            rows = pl.ds(pl.multiple_of(me * capacity + b * LANES, LANES), LANES)
+            back[rows, :] = gather(me, b)
+            return carry
+
+        lax.fori_loop(0, 1, keep, 0)
+        waiting.start()
+        lax.fori_loop(1, blocks, keep, 0)
         beside()
+        for (j, c), copy in zip(copies, started):
+            copy.wait_recv()
+
+            def restore(b, carry, j=j, c=c):
+                lanes = pl.ds(pl.multiple_of(b * LANES, LANES), LANES)
+                start = peers[j] * capacity + c * piece + b * LANES
+                columns = raw[j * PIECES + c, :, lanes]
+                rows = jnp.concatenate([columns, pad], axis=0).T
+                back[pl.ds(pl.multiple_of(start, LANES), LANES), :] = rows
+                return carry
+
+            lax.fori_loop(0, steps, restore, 0)
         for copy in started:
-            copy.wait()
+            copy.wait_send()
 
     def weights():
         for copy in loads[1] + loads[2]:
@@ -406,8 +454,8 @@
         fill_weight(first_ref, first_rows)
         fill_weight(second_ref, second_rows)
 
-    exchange(gather_1, 0, sent_1, back_1, weights)
-    exchange(gather_2, 1, sent_2, back_2, lambda: None)
+    exchange(gather_1, 0, sent_1, raw_1, back_1, weights)
+    exchange(gather_2, 1, sent_2, raw_2, back_2, lambda: None)
 
     def unpack(start):
         start = pl.multiple_of(start, LANES)
@@ -531,6 +579,7 @@
     rows = lambda count: pltpu.VMEM((count, width), jnp.float32)
     shape = lambda *dims: jax.ShapeDtypeStruct(dims, jnp.float32)
     edge = layers * components
+    columns = pltpu.VMEM((3 * PIECES, edge, capacity // PIECES), jnp.float32)
     return pl.pallas_call(
         functools.partial(exchange_kernel, layers, components, cross_dev, capacity),
         out_shape=[
@@ -551,8 +600,10 @@
             rows(cells),
             rows(cells),
             rows(cells),
-            rows(3 * capacity),
-            rows(3 * capacity),
+            columns,
+            columns,
+            columns,
+            columns,
             rows(4 * capacity),
             rows(4 * capacity),
             rows(LANES),

time: 170 us -> 157 us (0.924)
  between operations: 15 us -> 0.14 us
where the time goes in v4:
time: 157 us; the launch traced here: 155 us
  Pallas kernels  136 us (87%)
  other arithmetic  14.7 us (9%)
  local copies, waits for them, and re-layouts  3.97 us (3%)
    pallas_call x1, Pallas kernels, advect_twice(): pl.pallas_call(functools.partial(exchange_kernel, layers, components, cro...  126 us
    sort x2, other arithmetic, plan(): lax.sort(key[s]) % cells  11.6 us
    pallas_call x1, Pallas kernels, mix_and_solve(): pl.pallas_call(functools.partial(solve_kernel, layers, components), out_s...  8.37 us

profile of v4, /device:TPU:4, one launch (start us, length us, event | category | flops | bytes accessed | tf_op | source)
XLA Modules:
  0.0 155.1 jit_solution(8804462292531564271)
XLA Ops:
  0.0 0.1 eq.37
  0.1 0.7 broadcast_add_fusion.present_ref
  0.8 0.7 copy.12
  1.5 0.7 copy.13
  2.3 0.4 fusion.5
  2.7 5.8 %sort.29 = (s32[4096]{0:T(1024)S(1)}, s32[4096]{0:T(1024)}) sort(s32[4096]{0:T(1024)S(1)} %bitcast.22, s32[4096]{0:T(1024)S(1)} %iota.49), dimensions={0}, to_apply=%region_6.7 | sort | flops 49152 | bytes 65536 | tf_op jit(solution)/shard_map/sort | solution.py:134
  8.5 5.8 %sort.28 = (s32[4096]{0:T(1024)S(1)}, s32[4096]{0:T(1024)}) sort(s32[4096]{0:T(1024)S(1)} %bitcast.19, s32[4096]{0:T(1024)S(1)} %iota.48), dimensions={0}, to_apply=%region_5.6 | sort | flops 49152 | bytes 65536 | tf_op jit(solution)/shard_map/sort | solution.py:134
  14.4 0.7 reshape.204.ordered_ref
  15.1 0.1 eq.35
  15.2 0.3 convert_reduce_fusion
  15.5 0.2 reduce_window_sum.22
  15.7 0.2 fusion
  15.9 0.8 convert_reduce_fusion.1
  16.7 0.2 reduce_window_sum.23
  16.9 0.5 sub.41.starts_ref
  17.5 1.6 %cut_requests.1 = s32[4,2,9,128]{3,2,1,0:T(8,128)} custom-call(s32[2,4]{1,0:T(2,128)} %sub.41.starts_ref, s32[2,55,128]{2,1,0:T(8,128)} %reshape.204.ordered_ref), custom_call_target="tpu_custom_call" | custom-call | tf_op jit(solution)/shard_map/cut_requests/pallas_call | solution.py:108
  19.0 0.9 copy.10
  19.9 0.6 copy.11.requests_ref
  20.5 126.2 %advect_twice.1 = (f32[4,960,128]{2,1,0:T(8,128)}, f32[1,960,128]{2,1,0:T(8,128)}, f32[1,960,128]{2,1,0:T(8,128)}, f32[4,120,128]{2,1,0:T(8,128)}, f32[4,120,128]{2,1,0:T(8,128)}) custom-call(s32[2,4096]{1,0:T(2,128)} %get-tuple-element.22.target_ref, s32[4,18,128]{2,1,0:T(8,128)} %copy.11.requests_ref, f32[960,512]{1,0:T(8,128)} %bitcast.15, ...), custom_call_target="tpu_custom_call" | custom-call | tf_op jit(solution)/shard_map/advect_twice/pallas_call | solution.py:583
  146.8 8.4 %mix_and_solve.1 = f32[40,3,8,512]{3,2,1,0:T(8,128)} custom-call(f32[4,960,128]{2,1,0:T(8,128)} %get-tuple-element.16.moved_ref, f32[1,960,128]{2,1,0:T(8,128)} %get-tuple-element.17.west_ref, f32[1,960,128]{2,1,0:T(8,128)} %get-tuple-element.18.east_ref, f32[4,120,128]{2,1,0:T(8,128)} %get-tuple-element.19.north_ref, ...), custom_call_target="tpu_custom_call" | custom-call | tf_op jit(solution)/shard_map/mix_and_solve/pallas_call | solution.py:741
  (18 shorter events, 0.2 us)
